TPU v7x, 512 devices: a whole 4x8x8 slice. The times are simulated.
512 devices in a mesh: grow: 32 (over x_hi, y, core), gcol: 16 (over z, x_lo).
Axes of the slice: x: 4 (x_hi: 2, x_lo: 2; x = x_hi * 2 + x_lo), y: 8, z: 8, core: 2. Of those that a mesh axis runs over, the one named last changes fastest.
Arguments:
- coefficients: bfloat16 [20480, 49152], P('grow', 'gcol'), may hold values from -0.02734375 to 0.02734375
- tile_mask: int32 [160, 384], P('grow', 'gcol'), may hold values 0 or 1
- duals: float32 [20480], P('grow'), may hold values from -6 to 6
- costs: float32 [49152], P('gcol'), may hold values from -6 to 6
- primal: float32 [49152], P('gcol'), may hold values from 0.1 to 10
- fixed: int32 [49152], P('gcol'), may hold values 0 or 1
Outputs:
- normal_window: float32 [1024, 20480], P('gcol', 'grow')
- factor_window: float32 [1024, 20480], P('gcol', 'grow')
All inputs are finite; a program needn't handle non-finite values. No bound on the sum of `tile_mask` or of `fixed` on one device may be relied on, other than what follows from the above.
Results may differ from a plain program's by a relative error of at most 0.0023.
Values may be sent and summed in bfloat16 or wider, within the bound.
A program may use at most 64 MiB of HBM per device.

v0:
```python
import jax
import jax.numpy as jnp
from jax import lax
from jax.sharding import PartitionSpec as P

PANEL = 512


SOFTNESS = 0.25
DIAGONAL_SHIFT = 0.5


def split_normal(normal, blocks_own, panel_per, rows_dev):
    split = normal.reshape(blocks_own, 2, panel_per, rows_dev)
    own_panel = split[:, 0].reshape(blocks_own * panel_per, rows_dev)
    own_trailing = split[:, 1].reshape(blocks_own * panel_per, rows_dev)
    panel_all = lax.all_gather(own_panel, "gcol", axis=0, tiled=True)
    return (own_trailing, panel_all)


def shards(coefficients, tile_mask, duals, costs, primal, fixed):
    rows_dev, columns = coefficients.shape
    row_count = lax.axis_size("grow")
    col_count = lax.axis_size("gcol")
    panel_per = PANEL // row_count
    blocks_own = row_count // col_count
    local_win = blocks_own * 2 * panel_per
    tile_rows, tile_cols = tile_mask.shape
    side = rows_dev // tile_rows
    expanded = jnp.broadcast_to(
        tile_mask[:, None, :, None], (tile_rows, side, tile_cols, side)
    ).reshape(rows_dev, columns)
    masked = coefficients * expanded.astype(jnp.bfloat16)
    partial_products = jnp.dot(
        duals, masked, preferred_element_type=jnp.float32, precision=lax.Precision.HIGHEST
    )
    products = lax.psum(partial_products, "grow")
    reduced = costs - products
    scaling = (1 - fixed).astype(jnp.float32) * primal / jnp.sqrt(reduced * reduced + SOFTNESS)
    scaled = (masked * scaling[None, :]).astype(jnp.bfloat16)
    window_all = lax.all_gather(masked[: 2 * panel_per], "grow", axis=0, tiled=True)
    col_index = lax.axis_index("gcol")
    normal = lax.psum_scatter(
        lax.dot_general(
            window_all, scaled, (((1,), (1,)), ((), ())), preferred_element_type=jnp.float32
        ),
        "gcol",
        scatter_dimension=0,
        tiled=True,
    )
    own_trailing, panel_all = split_normal(normal, blocks_own, panel_per, rows_dev)
    corner = lax.all_gather(panel_all[:, :panel_per], "grow", axis=1, tiled=True)
    shifted = 0.5 * (corner + corner.T) + DIAGONAL_SHIFT * jnp.eye(PANEL, dtype=jnp.float32)
    lower = jnp.linalg.cholesky(shifted)
    factor_panel = jax.scipy.linalg.solve_triangular(lower, panel_all, lower=True)
    edge_all = lax.all_gather(
        factor_panel[:, panel_per : 2 * panel_per], "grow", axis=1, tiled=True
    )
    own_edge = lax.dynamic_slice_in_dim(
        edge_all, col_index * (blocks_own * panel_per), blocks_own * panel_per, 1
    )
    updated = own_trailing - jnp.dot(own_edge.T, factor_panel, precision=lax.Precision.HIGHEST)
    panel_rows = lax.dynamic_slice_in_dim(
        factor_panel, col_index * (blocks_own * panel_per), blocks_own * panel_per, 0
    )
    factor = jnp.stack(
        [
            panel_rows.reshape(blocks_own, panel_per, rows_dev),
            updated.reshape(blocks_own, panel_per, rows_dev),
        ],
        axis=1,
    )
    return (normal, factor.reshape(local_win, rows_dev))


def solution(mesh):
    placed = (P("grow", "gcol"), P("grow", "gcol"), P("grow"), P("gcol"), P("gcol"), P("gcol"))
    return jax.shard_map(
        shards,
        mesh=mesh,
        in_specs=placed,
        out_specs=(P("gcol", "grow"), P("gcol", "grow")),
        check_vma=False,
    )
```

profile of v0, /device:TPU:6, one launch (start us, length us, event | category | flops | bytes accessed | tf_op | source)
XLA Modules:
  0.0 639.5 jit_solution(5346488050266648543)
XLA Ops:
  7.2 0.8 convert_element_type.17
  8.1 0.6 broadcast_in_dim.3
  8.6 0.7 copy-done.2
  9.3 0.5 bitcast_multiply_fusion
  9.9 1.9 copy-done
  11.8 0.7 slice.145
  12.6 3.7 fusion.38
  16.3 132.8 %psum.7 = f32[3072]{0:T(1024)S(1)} all-reduce(f32[3072]{0:T(1024)S(1)} %bitcast.77), channel_id=1, replica_groups=mesh['grow'=32,'gcol'=16] {'grow'}, use_global_device_ids=true, to_apply=%region_0.0 | all-reduce | flops 3072 | bytes 24576 | tf_op jit(solution)/shard_map/psum | solution.py:37
  149.1 9.5 %fusion = f32[1024,640]{1,0:T(8,128)} fusion(bf16[1024,3072]{1,0:T(8,128)(2,1)} %all-gather.5.cloned.1.call-done, bf16[640,3072]{1,0:T(8,128)(2,1)} %copy-done, f32[3072]{0:T(1024)S(1)} %rsqrt_multiply_fusion), kind=kOutput, calls=%fused_computation.3 | convolution fusion | flops 4032430080 | bytes 12857344 | tf_op jit(solution)/shard_map/dot_general | solution.py:44
  158.7 78.7 %reduce-scatter.2.cloned.1.call-done = f32[64,640]{1,0:T(8,128)} async-done(((f32[1024,640]{1,0:T(8,128)}), f32[64,640]{1,0:T(8,128)}) %reduce-scatter.2.cloned.1.call-update) | async-done | bytes 163856 | tf_op jit(solution)/shard_map/reduce_scatter | solution.py:43
  237.4 1.6 fusion.37
  239.0 73.4 %all-gather.7.cloned.1.call-done = f32[512,640]{1,0:T(8,128)} async-done(((f32[32,640]{1,0:T(8,128)}), f32[512,640]{1,0:T(8,128)}) %all-gather.7.cloned.1.call-update) | async-done | bytes 1310736 | tf_op jit(solution)/shard_map/all_gather | solution.py:17
  312.5 1.0 slice.147
  313.4 0.7 copy.24
  314.2 0.5 all-gather.11.cloned.1.call-start
  314.7 83.0 %all-gather.9.cloned.1.call-done = f32[512,512]{0,1:T(8,128)} async-done(((f32[512,16]{0,1:T(8,128)}), f32[512,512]{0,1:T(8,128)}) %all-gather.9.cloned.1.call-update) | async-done | bytes 1048592 | tf_op jit(solution)/shard_map/all_gather | solution.py:52
  397.7 1.6 copy.19
  399.4 0.2 fusion.4
  399.6 0.3 copy.20
  399.9 0.2 fusion.2
  400.2 11.7 %cholesky.103 = f32[128,128]{1,0:T(8,128)S(1)} custom-call(f32[128,128]{1,0:T(8,128)S(1)} %cholesky.263), custom_call_target="Cholesky" | custom-call | tf_op jit(solution)/shard_map/jit(cholesky)/cholesky | solution.py:54
  411.9 9.8 %custom-call.31 = f32[1,128,128]{1,2,0:T(8,128)S(1)} custom-call(f32[1,128,128]{2,1,0:T(8,128)S(1)} %get-tuple-element.31), custom_call_target="InvertDiagBlocksLowerTriangular" | custom-call | tf_op jit(solution)/shard_map/jit(cholesky)/cholesky | solution.py:54
  421.8 0.1 cholesky.222
  421.9 0.3 constant_dynamic-update-slice_fusion.2
  422.2 1.0 convolution_subtract_fusion.3
  423.2 0.9 cholesky.267
  424.2 11.7 %cholesky.215 = f32[128,128]{1,0:T(8,128)S(1)} custom-call(f32[128,128]{1,0:T(8,128)S(1)} %cholesky.267), custom_call_target="Cholesky" | custom-call | tf_op jit(solution)/shard_map/jit(cholesky)/cholesky | solution.py:54
  435.9 9.9 %custom-call.32 = f32[1,128,128]{1,2,0:T(8,128)S(1)} custom-call(f32[1,128,128]{2,1,0:T(8,128)S(1)} %get-tuple-element.28), custom_call_target="InvertDiagBlocksLowerTriangular" | custom-call | tf_op jit(solution)/shard_map/jit(cholesky)/cholesky | solution.py:54
  445.9 1.2 convolution_dynamic-update-slice_fusion
  447.0 0.4 convolution_subtract_fusion.4
  447.4 0.6 cholesky.272
  448.1 13.2 %cholesky.236 = f32[128,128]{1,0:T(8,128)} custom-call(f32[128,128]{1,0:T(8,128)} %cholesky.272), custom_call_target="Cholesky" | custom-call | tf_op jit(solution)/shard_map/jit(cholesky)/cholesky | solution.py:54
  461.2 1.5 select_reduce_fusion.1
  462.7 0.7 compare_reduce_fusion.1
  463.4 11.3 %custom-call.33 = f32[1,128,128]{1,2,0:T(8,128)} custom-call(f32[1,128,128]{2,1,0:T(8,128)} %get-tuple-element.25), custom_call_target="InvertDiagBlocksLowerTriangular" | custom-call | tf_op jit(solution)/shard_map/jit(cholesky)/cholesky | solution.py:54
  474.7 1.0 convolution_dynamic-update-slice_fusion.1
  475.7 0.4 convolution_subtract_fusion.6
  476.1 11.9 %cholesky.253 = f32[128,128]{1,0:T(8,128)S(1)} custom-call(f32[128,128]{1,0:T(8,128)S(1)} %convolution_subtract_fusion.6), custom_call_target="Cholesky" | custom-call | tf_op jit(solution)/shard_map/jit(cholesky)/cholesky | solution.py:54
  488.1 0.7 compare_reduce_fusion
  488.8 0.6 compare_reduce_fusion.2
  491.9 0.1 select_select_fusion
  492.0 10.7 %while.1 = (s32[]{:T(128)}, f32[512,512]{1,0:T(8,128)S(1)}, s32[4,2]{0,1:T(2,128)S(1)}, f32[4,128,128]{2,1,0:T(8,128)}, s32[]{:T(128)}) while((s32[]{:T(128)}, f32[512,512]{1,0:T(8,128)S(1)}, s32[4,2]{0,1:T(2,128)S(1)}, f32[4,128,128]{2,1,0:T(8,128)}, s32[]{:T(128)}) %tuple.32), condition=%wide.while_cond, body=%wide.while_body.sunk | while | flops 2 | bytes 132705 | solution.py:55
  492.1 0.6 fusion.48
  492.7 2.0 bitcast_dynamic-update-slice_fusion.2
  494.8 0.6 fusion.48
  495.4 2.0 bitcast_dynamic-update-slice_fusion.2
  497.4 0.6 fusion.48
  498.0 2.0 bitcast_dynamic-update-slice_fusion.2
  500.1 0.6 fusion.48
  500.7 2.0 bitcast_dynamic-update-slice_fusion.2
  502.7 40.1 %custom-call.34 = f32[4,128,128]{1,2,0:T(8,128)S(1)} custom-call(f32[4,128,128]{2,1,0:T(8,128)} %get-tuple-element.9), custom_call_target="InvertDiagBlocksLowerTriangular" | custom-call | tf_op jit(solution)/shard_map/jit(_solve_triangular)/triangular_solve | solution.py:55
  542.8 0.5 fusion.13
  543.3 0.2 copy-done.4
  543.5 0.4 convolution_subtract_fusion.1
  543.9 1.3 fusion.26
  545.2 0.5 convolution_subtract_fusion
  545.8 1.3 fusion.24
  547.1 0.9 convolution_subtract_fusion.2
  548.0 1.3 fusion.23
  549.4 0.1 slice.149
  549.6 0.7 copy.21
  550.3 80.1 %all-gather.11.cloned.1.call-done = f32[512,512]{0,1:T(8,128)} async-done(((f32[512,16]{0,1:T(8,128)}), f32[512,512]{0,1:T(8,128)}) %all-gather.11.cloned.1.call-update) | async-done | bytes 1048592 | tf_op jit(solution)/shard_map/all_gather | solution.py:56
  630.4 1.7 convolution_subtract_fusion.5
  632.1 0.7 copy.22
  (43 shorter events, 0.8 us)
Async XLA Ops:
  7.2 142.0 %all-gather.5.cloned.1.call-start = ((), (), s32[]{:S(2)}) async-start(), calls=%async_computation.1 | async-start | bytes 6488064 | tf_op jit(solution)/shard_map/all_gather | solution.py:41
  7.2 2.1 copy-start.2
  9.3 3.2 copy-start.9
  9.9 1.9 copy-start
  11.8 137.3 %copy-start.6 = (f32[3072]{0:T(1024)S(1)}, f32[3072]{0:T(1024)}, u32[]{:S(2)}) copy-start(f32[3072]{0:T(1024)} %param.9) | copy-start | bytes 36868
  11.8 137.3 %copy-start.7 = (f32[3072]{0:T(1024)S(1)}, f32[3072]{0:T(1024)}, u32[]{:S(2)}) copy-start(f32[3072]{0:T(1024)} %param.10) | copy-start | bytes 36868
  11.8 137.3 %copy-start.8 = (s32[3072]{0:T(1024)S(1)}, s32[3072]{0:T(1024)}, u32[]{:S(2)}) copy-start(s32[3072]{0:T(1024)} %param.11) | copy-start | bytes 36868
  12.5 224.9 %reduce-scatter.2.cloned.1.call-start = ((), (), s32[]{:S(2)}) async-start(), calls=%async_computation.2 | async-start | bytes 2785280 | tf_op jit(solution)/shard_map/reduce_scatter | solution.py:43
  158.6 153.8 %all-gather.7.cloned.1.call-start = ((), (), s32[]{:S(2)}) async-start(), calls=%async_computation.3 | async-start | bytes 1392640 | tf_op jit(solution)/shard_map/all_gather | solution.py:17
  239.0 158.7 %all-gather.9.cloned.1.call-start = ((), (), s32[]{:S(2)}) async-start(), calls=%async_computation.4 | async-start | bytes 1081344 | tf_op jit(solution)/shard_map/all_gather | solution.py:52
  314.2 316.2 %all-gather.11.cloned.1.call-start = ((), (), s32[]{:S(2)}) async-start(), calls=%async_computation.5 | async-start | bytes 1081344 | tf_op jit(solution)/shard_map/all_gather | solution.py:56
  397.7 1.7 copy-start.1
  423.2 119.6 %copy-start.3 = (f32[512,640]{1,0:T(8,128)S(1)}, f32[512,640]{1,0:T(8,128)}, u32[]{:S(2)}) copy-start(f32[512,640]{1,0:T(8,128)} %all-gather.7.cloned.1.call-done) | copy-start | bytes 3932164
  542.8 0.7 copy-start.4
  548.0 82.4 %copy-start.5 = (f32[2,1,16,640]{3,2,1,0:T(8,128)S(1)}, f32[2,1,16,640]{3,2,1,0:T(8,128)}, u32[]{:S(2)}) copy-start(f32[2,1,16,640]{3,2,1,0:T(8,128)} %get-tuple-element.21) | copy-start | bytes 245764
Sparse Core Ops, SparseCore 0:
  12.6 102.8 all-gather.4
  158.8 78.5 reduce-scatter.1
  240.0 72.3 all-gather.6
  316.3 81.4 all-gather.8
  550.4 79.9 all-gather.10
where the time goes:
time: 648 us; the launch traced here: 640 us
  waiting for transfers between devices  315 us (49%)
  blocking collectives  133 us (21%)
  other arithmetic  125 us (19%)
  matrix products  25.4 us (4%)
  local copies, waits for them, and re-layouts  23.3 us (4%)
  between operations  16.8 us (3%)
    psum x1, blocking collectives, shards(): products = lax.psum(partial_products, 'grow')  133 us
    another operation x14, other arithmetic, shards(): lower = jnp.linalg.cholesky(shifted)  83.1 us
    all_gather x1, waiting for transfers between devices, shards(): lax.all_gather(panel_all[:, :panel_per], 'grow', axis=1, tiled=True)  83 us
    all_gather x1, waiting for transfers between devices, shards(): lax.all_gather(factor_panel[:, panel_per:2 * panel_per], 'grow', axis=1,...  80.1 us
    reduce_scatter x1, waiting for transfers between devices, shards(): lax.psum_scatter(lax.dot_general(window_all, scaled, (((1,), (1,)), ((),...  78.7 us
    all_gather x1, waiting for transfers between devices, split_normal(): panel_all = lax.all_gather(own_panel, 'gcol', axis=0, tiled=True)  73.4 us
    another operation x4, other arithmetic, shards(): jax.scipy.linalg.solve_triangular(lower, panel_all, lower=True)  40.3 us
  transfers between devices with their start and end apart: 5, of which 4 were waited for; matrix products, arithmetic and copies ran while one was open for 1% of the time, Pallas kernels for 0%

commit v1 on v0

v1 whole, which is shorter than its diff:
```python
import functools

import jax
import jax.numpy as jnp
from jax import lax
from jax.experimental import pallas as pl
from jax.experimental.pallas import tpu as pltpu
from jax.sharding import PartitionSpec as P

PANEL = 512
SOFTNESS = 0.25
DIAGONAL_SHIFT = 0.5
CORES = 2
PLANES = 2
BLOCK = 128
MESH = pl.DeviceIdType.MESH
HIGHEST = lax.Precision.HIGHEST
NT = (((1,), (1,)), ((), ()))


def copy_to(src, dst, send_sem, recv_sem, g, c):
    return pltpu.make_async_remote_copy(
        src_ref=src, dst_ref=dst, send_sem=send_sem, recv_sem=recv_sem, device_id=(g, c), device_id_type=MESH
    )


class Place:
    def __init__(self, row_count, col_count):
        self.y_count = row_count // (CORES * PLANES)
        self.row_count, self.col_count = row_count, col_count
        self.g = lax.axis_index("grow")
        self.c = lax.axis_index("gcol")
        self.core = lax.rem(self.g, CORES)
        chip = self.g // CORES
        self.y = lax.rem(chip, self.y_count)
        self.plane = chip // self.y_count

    def at(self, plane, y, core):
        return (plane * self.y_count + y) * CORES + core

    def ring(self, hop):
        return lax.rem(self.y + hop + 2 * self.y_count, self.y_count)


def enter(me, wait):
    barrier = pltpu.get_barrier_semaphore()
    if not wait:
        for k in range(1, me.row_count):
            pl.semaphore_signal(
                barrier, inc=1, device_id=(lax.rem(me.g + k, me.row_count), me.c), device_id_type=MESH
            )
        for k in range(1, me.col_count):
            pl.semaphore_signal(
                barrier, inc=1, device_id=(me.g, lax.rem(me.c + k, me.col_count)), device_id_type=MESH
            )
    else:
        pl.semaphore_wait(barrier, me.row_count + me.col_count - 2)


def window_kernel(
    row_count, col_count, panel_per,
    coef, mask, duals, costs, primal, fixed,
    normal,
    a, win, dcol, pa, pb, scale, part, own, out, inc,
    load_sem, win_send, win_recv, pa_send, pa_recv, pb_send, pb_recv, rs_send, rs_recv,
):
    me = Place(row_count, col_count)
    rows, columns = a.shape
    window = 2 * panel_per
    tile_rows, tile_cols = mask.shape
    side = rows // tile_rows
    yc = me.y_count

    enter(me, False)
    first = pltpu.make_async_copy(coef.at[pl.ds(0, window)], a.at[pl.ds(0, window)], load_sem.at[0])
    rest = pltpu.make_async_copy(
        coef.at[pl.ds(window, rows - window)], a.at[pl.ds(window, rows - window)], load_sem.at[1]
    )
    first.start()
    rest.start()
    first.wait()

    def mask_window(k, _):
        sl = pl.ds(pl.multiple_of(k * side, side), side)
        m = mask[0, k].astype(jnp.float32)
        win[me.g, :, sl] = (a[0:window, sl].astype(jnp.float32) * m).astype(jnp.bfloat16)
        return 0

    lax.fori_loop(0, tile_cols, mask_window, 0)
    enter(me, True)

    sends = []

    def send_window(slot, g, c):
        cp = copy_to(win.at[slot], win.at[slot], win_send.at[len(sends)], win_recv.at[slot], g, c)
        cp.start()
        sends.append(cp)

    def got_window(slot):
        copy_to(win.at[slot], win.at[slot], win_send.at[0], win_recv.at[slot], me.g, me.c).wait_recv()

    sibling = me.at(me.plane, me.y, 1 - me.core)
    right = me.at(me.plane, me.ring(1), me.core)
    left = me.at(me.plane, me.ring(-1), me.core)
    other = 1 - me.plane
    reach = {0: (yc // 2, (yc - 1) // 2), 1: ((yc - 1) // 2, yc // 2)}

    def pass_on(kind, hop_right, hop_left, which):
        plane = me.plane if kind == 0 else other
        if which in (0, 1) and hop_right < reach[kind][0]:
            send_window(me.at(plane, me.ring(-hop_right), me.core), right, me.c)
        if which in (0, 2) and hop_left < reach[kind][1]:
            send_window(me.at(plane, me.ring(hop_left), me.core), left, me.c)

    send_window(me.g, me.at(other, me.y, me.core), me.c)
    pass_on(0, 0, 0, 0)
    send_window(me.g, sibling, me.c)

    for i in range(tile_rows):
        dcol[i * side:(i + 1) * side, :] = jnp.transpose(jnp.broadcast_to(duals[i:i + 1, :], (side, side)))
    rest.wait()
    q = me.plane * CORES + me.core

    def products(k, _):
        sl = pl.ds(pl.multiple_of(k * side, side), side)
        total = jnp.zeros((8, side), jnp.float32)
        for i in range(tile_rows):
            block = slice(i * side, (i + 1) * side)
            x = a[block, sl].astype(jnp.float32) * mask[i, k].astype(jnp.float32)
            a[block, sl] = x.astype(jnp.bfloat16)
            total += (x * dcol[block, :]).reshape(side // 8, 8, side).sum(axis=0)
        pa[q, :, sl] = total.sum(axis=0, keepdims=True)
        return 0

    lax.fori_loop(0, tile_cols, products, 0)

    small = []
    n = 0
    for dp in range(PLANES):
        for dc in range(CORES):
            if dp == 0 and dc == 0:
                continue
            plane = lax.rem(me.plane + dp, PLANES)
            core = lax.rem(me.core + dc, CORES)
            cp = copy_to(pa.at[q], pa.at[q], pa_send.at[n], pa_recv.at[q], me.at(plane, me.y, core), me.c)
            cp.start()
            small.append(cp)
            n += 1

    partner = me.at(other, me.y, me.core)
    got_window(partner)
    pass_on(1, 0, 0, 0)
    send_window(partner, sibling, me.c)

    for dp in range(PLANES):
        for dc in range(CORES):
            if dp == 0 and dc == 0:
                continue
            s = lax.rem(me.plane + dp, PLANES) * CORES + lax.rem(me.core + dc, CORES)
            copy_to(pa.at[s], pa.at[s], pa_send.at[0], pa_recv.at[s], me.g, me.c).wait_recv()
    total = pa[0]
    for s in range(1, PLANES * CORES):
        total = total + pa[s]
    pb[me.y] = total
    for k in range(1, yc):
        cp = copy_to(
            pb.at[me.y], pb.at[me.y], pb_send.at[k], pb_recv.at[me.y], me.at(me.plane, me.ring(k), me.core), me.c
        )
        cp.start()
        small.append(cp)

    def service(hop):
        for kind in (0, 1):
            plane = me.plane if kind == 0 else other
            if hop <= reach[kind][0]:
                slot = me.at(plane, me.ring(-hop), me.core)
                got_window(slot)
                pass_on(kind, hop, 0, 1)
                send_window(slot, sibling, me.c)
            if hop <= reach[kind][1]:
                slot = me.at(plane, me.ring(hop), me.core)
                got_window(slot)
                pass_on(kind, 0, hop, 2)
                send_window(slot, sibling, me.c)

    service(1)
    for k in range(1, yc):
        s = me.ring(k)
        copy_to(pb.at[s], pb.at[s], pb_send.at[0], pb_recv.at[s], me.g, me.c).wait_recv()
    total = pb[0]
    for s in range(1, yc):
        total = total + pb[s]
    reduced = costs[...] - total
    scale[...] = (1 - fixed[...]).astype(jnp.float32) * primal[...] / jnp.sqrt(reduced * reduced + SOFTNESS)

    def rescale(k, _):
        sl = pl.ds(pl.multiple_of(k * side, side), side)
        s = jnp.broadcast_to(scale[:, sl], (side, side))
        for i in range(tile_rows):
            block = slice(i * side, (i + 1) * side)
            a[block, sl] = (a[block, sl].astype(jnp.float32) * s).astype(jnp.bfloat16)
        return 0

    lax.fori_loop(0, tile_cols, rescale, 0)
    for hop in range(2, yc // 2 + 1):
        service(hop)
    for plane in range(PLANES):
        for y in range(yc):
            got_window(me.at(plane, y, 1 - me.core))

    owners = min(4, col_count)
    groups = col_count // owners
    blocks = row_count // col_count
    mine = blocks * window
    depth = min(512, columns)
    inc[me.c] = jnp.zeros(inc.shape[1:], inc.dtype)

    def multiply(step, _):
        group = lax.rem(me.c // owners + step, groups)
        part[...] = jnp.zeros_like(part)

        def deep(k, _):
            sl = pl.ds(pl.multiple_of(k * depth, depth), depth)
            lhs = win[pl.ds(group * (owners * blocks), owners * blocks), :, sl].reshape(owners * mine, depth)
            part[...] += lax.dot_general(lhs, a[:, sl], NT, preferred_element_type=jnp.float32)
            return 0

        lax.fori_loop(0, columns // depth, deep, 0)
        for k in range(owners):
            owner = group * owners + k
            piece = part[k * mine:(k + 1) * mine, :]
            out[owner] = piece.astype(jnp.bfloat16)

            @pl.when(owner == me.c)
            def _():
                own[...] = piece

            @pl.when(owner != me.c)
            def _():
                copy_to(out.at[owner], inc.at[me.c], rs_send.at[owner], rs_recv.at[me.c], me.g, owner).start()

        return 0

    lax.fori_loop(0, groups, multiply, 0)
    for s in range(col_count):
        @pl.when(me.c != s)
        def _():
            copy_to(out.at[s], inc.at[s], rs_send.at[s], rs_recv.at[s], me.g, me.c).wait_recv()

    total = own[...]
    for s in range(col_count):
        total = total + inc[s].astype(jnp.float32)
    normal[...] = total

    for s in range(col_count):
        @pl.when(me.c != s)
        def _():
            copy_to(out.at[s], inc.at[s], rs_send.at[s], rs_recv.at[s], me.g, me.c).wait_send()
    for cp in small + sends:
        cp.wait_send()


def gather_kernel(
    row_count, col_count, panel_per,
    normal,
    panel, corner, edge,
    epiece, panel_send, panel_recv, corner_send, corner_recv, edge_send, edge_recv,
):
    me = Place(row_count, col_count)
    blocks = row_count // col_count
    enter(me, False)
    for b in range(blocks):
        panel[me.c, b * panel_per:(b + 1) * panel_per, :] = normal[2 * b * panel_per:(2 * b + 1) * panel_per, :]
    enter(me, True)
    sends = []
    for k in range(1, col_count):
        cp = copy_to(
            panel.at[me.c], panel.at[me.c], panel_send.at[k], panel_recv.at[me.c],
            me.g, lax.rem(me.c + k, col_count),
        )
        cp.start()
        sends.append(cp)
    for k in range(1, col_count):
        s = lax.rem(me.c + k, col_count)
        copy_to(panel.at[s], panel.at[s], panel_send.at[0], panel_recv.at[s], me.g, me.c).wait_recv()
    head = panel[:, :, 0:BLOCK].reshape(panel.shape[0] * panel.shape[1], BLOCK)
    turned = jnp.transpose(head)
    corner[me.g] = turned[0:panel_per]
    epiece[...] = turned[panel_per:2 * panel_per]
    sibling = me.at(me.plane, me.y, 1 - me.core)

    def send_corner(slot, g):
        cp = copy_to(corner.at[slot], corner.at[slot], corner_send.at[len(sends) - col_count + 1], corner_recv.at[slot], g, me.c)
        cp.start()
        sends.append(cp)

    peers = [
        me.at(lax.rem(me.plane + p, PLANES), me.ring(k), me.core)
        for k in range(me.y_count) for p in range(PLANES) if k or p
    ]
    for peer in peers:
        send_corner(me.g, peer)
    send_corner(me.g, sibling)

    source = me.g // CORES == me.c

    def edge_copy(n, g):
        return copy_to(edge.at[me.core], edge.at[me.core], edge_send.at[n], edge_recv.at[me.core], g, me.c)

    @pl.when(source)
    def _():
        edge[me.core] = epiece[...]
        for n, peer in enumerate(peers):
            edge_copy(n, peer).start()

    @pl.when(jnp.logical_not(source))
    def _():
        edge_copy(0, me.g).wait_recv()

    edge_copy(len(peers), sibling).start()

    for peer in peers:
        copy_to(corner.at[peer], corner.at[peer], corner_send.at[0], corner_recv.at[peer], me.g, me.c).wait_recv()
        send_corner(peer, sibling)
    for plane in range(PLANES):
        for y in range(me.y_count):
            s = me.at(plane, y, 1 - me.core)
            copy_to(corner.at[s], corner.at[s], corner_send.at[0], corner_recv.at[s], me.g, me.c).wait_recv()
    other = 1 - me.core
    copy_to(edge.at[other], edge.at[other], edge_send.at[0], edge_recv.at[other], me.g, me.c).wait_recv()

    @pl.when(source)
    def _():
        for n, peer in enumerate(peers):
            edge_copy(n, peer).wait_send()

    edge_copy(len(peers), sibling).wait_send()
    for cp in sends:
        cp.wait_send()


def invert_block(d):
    n = d.shape[0]
    lane = lax.broadcasted_iota(jnp.int32, (8, n), 1)
    sub = lax.broadcasted_iota(jnp.int32, (8, n), 0)
    rows = [d[8 * i:8 * i + 8, :] for i in range(n // 8)]
    pivots = []
    for b in range(n // 8):
        pivot = jnp.ones((8, n), jnp.float32)
        for s in range(8):
            j = 8 * b + s
            row = rows[b][s:s + 1, :]
            p = jnp.broadcast_to(rows[b][s:s + 1, j:j + 1], (1, n))
            row = jnp.where(lane[0:1] == j, 1.0, row) / p
            row = jnp.broadcast_to(row, (8, n))
            pivot = jnp.where(sub == s, jnp.broadcast_to(p, (8, n)), pivot)
            for i in range(b, n // 8):
                col = jnp.broadcast_to(rows[i][:, j:j + 1], (8, n))
                gone = lane == j
                if i == b:
                    col = jnp.where(sub > s, col, 0.0)
                    gone = gone & (sub > s)
                rows[i] = jnp.where(gone, 0.0, rows[i]) - col * row
        pivots.append(pivot)
    done = []
    for b in range(n // 8):
        r = sub + 8 * b
        low = jnp.where(lane < r, rows[b], jnp.where(lane == r, 1.0, 0.0))
        done.append(low / jnp.sqrt(pivots[b]))
    return jnp.concatenate(done, axis=0)


def dot32(x, y, dims=(((1,), (0,)), ((), ()))):
    return lax.dot_general(x, y, dims, precision=HIGHEST, preferred_element_type=jnp.float32)


def factor_kernel(col_count, panel_per, normal, panel, corner, edge, factor, s):
    n = s.shape[0]
    c = lax.axis_index("gcol")
    own = n // col_count
    row_id = lax.broadcasted_iota(jnp.int32, (n, n), 0)
    col_id = lax.broadcasted_iota(jnp.int32, (n, n), 1)
    given = corner[...]
    s[...] = 0.5 * (given + jnp.transpose(given)) + jnp.where(row_id == col_id, DIAGONAL_SHIFT, 0.0)

    def step(k, _):
        at = pl.ds(pl.multiple_of(k * BLOCK, BLOCK), BLOCK)
        inverse = invert_block(s[at, at])
        below = lax.broadcasted_iota(jnp.int32, (n, BLOCK), 0) >= (k + 1) * BLOCK
        column = jnp.where(below, dot32(s[:, at], inverse, NT), 0.0)
        s[at, at] = jnp.where(
            lax.broadcasted_iota(jnp.int32, (BLOCK, BLOCK), 0) == lax.broadcasted_iota(jnp.int32, (BLOCK, BLOCK), 1),
            1.0, 0.0,
        )
        row = dot32(inverse, s[at, :])
        s[at, :] = row
        s[:, at] = jnp.where(below, 0.0, s[:, at])
        s[...] = s[...] - dot32(column, row)
        return 0

    lax.fori_loop(0, n // BLOCK, step, 0)
    s[...] = jnp.where(col_id <= row_id, s[...], 0.0)
    inverse = s[...]
    turned_edge = dot32(edge[...], inverse, NT)
    weights = jnp.concatenate(
        [s[pl.ds(pl.multiple_of(c * own, own), own), :], dot32(turned_edge, inverse)], axis=0
    )
    made = dot32(weights, panel[...])
    for b in range(own // panel_per):
        at = b * panel_per
        factor[2 * at:2 * at + panel_per, :] = made[at:at + panel_per]
        factor[2 * at + panel_per:2 * at + 2 * panel_per, :] = (
            normal[2 * at + panel_per:2 * at + 2 * panel_per, :] - made[own + at:own + at + panel_per]
        )


def shards(row_count, col_count, coefficients, tile_mask, duals, costs, primal, fixed):
    rows, columns = coefficients.shape
    panel_per = PANEL // row_count
    window = 2 * panel_per
    blocks = row_count // col_count
    mine = blocks * window
    y_count = row_count // (CORES * PLANES)
    vmem, smem, anywhere = (pl.BlockSpec(memory_space=m) for m in (pltpu.VMEM, pltpu.SMEM, pl.ANY))
    dma = pltpu.SemaphoreType.DMA
    f32, bf16 = jnp.float32, jnp.bfloat16
    normal = pl.pallas_call(
        functools.partial(window_kernel, row_count, col_count, panel_per),
        out_shape=jax.ShapeDtypeStruct((mine, rows), f32),
        in_specs=[anywhere, smem, vmem, vmem, vmem, vmem],
        out_specs=vmem,
        scratch_shapes=[
            pltpu.VMEM((rows, columns), bf16),
            pltpu.VMEM((row_count, window, columns), bf16),
            pltpu.VMEM((rows, BLOCK), f32),
            pltpu.VMEM((PLANES * CORES, 1, columns), f32),
            pltpu.VMEM((y_count, 1, columns), f32),
            pltpu.VMEM((1, columns), f32),
            pltpu.VMEM((min(4, col_count) * mine, rows), f32),
            pltpu.VMEM((mine, rows), f32),
            pltpu.VMEM((col_count, mine, rows), bf16),
            pltpu.VMEM((col_count, mine, rows), bf16),
            dma((2,)),
            dma((2 * row_count,)), dma((row_count,)),
            dma((PLANES * CORES,)), dma((PLANES * CORES,)),
            dma((y_count,)), dma((y_count,)),
            dma((col_count,)), dma((col_count,)),
        ],
        compiler_params=pltpu.CompilerParams(collective_id=0, has_side_effects=True, vmem_limit_bytes=40 << 20),
        name="window",
    )(
        coefficients, tile_mask, duals.reshape(rows // BLOCK, BLOCK), costs.reshape(1, columns),
        primal.reshape(1, columns), fixed.reshape(1, columns),
    )
    own = PANEL // col_count
    panel, corner, edge = pl.pallas_call(
        functools.partial(gather_kernel, row_count, col_count, panel_per),
        out_shape=(
            jax.ShapeDtypeStruct((col_count, own, rows), f32),
            jax.ShapeDtypeStruct((row_count, panel_per, PANEL), f32),
            jax.ShapeDtypeStruct((blocks, panel_per, PANEL), f32),
        ),
        in_specs=[vmem],
        out_specs=(vmem, vmem, vmem),
        scratch_shapes=[
            pltpu.VMEM((panel_per, PANEL), f32),
            dma((col_count,)), dma((col_count,)),
            dma((row_count + 1,)), dma((row_count,)),
            dma((row_count // 2,)), dma((CORES,)),
        ],
        compiler_params=pltpu.CompilerParams(collective_id=1, has_side_effects=True, vmem_limit_bytes=24 << 20),
        name="gather",
    )(normal)
    factor = pl.pallas_call(
        functools.partial(factor_kernel, col_count, panel_per),
        out_shape=jax.ShapeDtypeStruct((mine, rows), f32),
        in_specs=[vmem] * 4,
        out_specs=vmem,
        scratch_shapes=[pltpu.VMEM((PANEL, PANEL), f32)],
        compiler_params=pltpu.CompilerParams(vmem_limit_bytes=32 << 20),
        name="factor",
    )(normal, panel.reshape(PANEL, rows), corner.reshape(PANEL, PANEL), edge.reshape(own, PANEL))
    return normal, factor


def solution(mesh):
    placed = (P("grow", "gcol"), P("grow", "gcol"), P("grow"), P("gcol"), P("gcol"), P("gcol"))
    return jax.shard_map(
        functools.partial(shards, mesh.shape["grow"], mesh.shape["gcol"]),
        mesh=mesh,
        in_specs=placed,
        out_specs=(P("gcol", "grow"), P("gcol", "grow")),
        check_vma=False,
    )
```

time: 648 us -> 209 us (0.32); the launches traced: 640 us -> 208 us
  waiting for transfers between devices: 315 us -> 0 us
  Pallas kernels: 0 us -> 201 us
  blocking collectives: 133 us -> 0 us
  other arithmetic: 125 us -> 0 us
  matrix products: 25.4 us -> 0 us
  local copies, waits for them, and re-layouts: 23.3 us -> 6.26 us
  between operations: 16.8 us -> 0.66 us
    all_gather x4 -> x0, waiting for transfers between devices: 237 us -> none  [the longest x1 83 us: shards(): lax.all_gather(panel_all[:, :panel_per], 'grow', axis=1, tiled=True)]
    pallas_call x0 -> x3, Pallas kernels: none -> 201 us  [the longest x1 91.3 us: shards(): pl.pallas_call(functools.partial(window_kernel, row_count, col_count, pan...]
    psum x1 -> x0, blocking collectives: 133 us -> none  [shards(): products = lax.psum(partial_products, 'grow')]
    another operation x19 -> x0, other arithmetic: 123 us -> none  [the longest x14 83.1 us: shards(): lower = jnp.linalg.cholesky(shifted)]
    reduce_scatter x1 -> x0, waiting for transfers between devices: 78.7 us -> none  [shards(): lax.psum_scatter(lax.dot_general(window_all, scaled, (((1,), (1,)), ((),...]
    dot_general x3 -> x0, matrix products: 14.9 us -> none  [the longest x1 9.47 us: shards(): lax.dot_general(window_all, scaled, (((1,), (1,)), ((), ())), preferred_e...]
    another operation x18 -> x0, local copies, waits for them, and re-layouts: 13 us -> none
    another operation x13 -> x0, matrix products: 10.5 us -> none  [the longest x7 6.24 us: shards(): jax.scipy.linalg.solve_triangular(lower, panel_all, lower=True)]
  transfers between devices with their start and end apart: 5 -> 0, of which waited for: 4 -> 0; matrix products, arithmetic and copies ran while one was open for 1% -> 0% of each run, Pallas kernels for 0% -> 0%
where the time goes in v1:
time: 209 us; the launch traced here: 208 us
  Pallas kernels  201 us (96%)
  local copies, waits for them, and re-layouts  6.26 us (3%)
    pallas_call x1, Pallas kernels, shards(): pl.pallas_call(functools.partial(window_kernel, row_count, col_count, pan...  91.3 us
    pallas_call x1, Pallas kernels, shards(): pl.pallas_call(functools.partial(gather_kernel, row_count, col_count, pan...  57.6 us
    pallas_call x1, Pallas kernels, shards(): pl.pallas_call(functools.partial(factor_kernel, col_count, panel_per), ou...  52.4 us
    unnamed x13, local copies, waits for them, and re-layouts  6.26 us

profile of v1, /device:TPU:6, one launch (start us, length us, event | category | flops | bytes accessed | tf_op | source)
XLA Modules:
  0.0 208.2 jit_solution(16363138777313649930)
XLA Ops:
  0.6 0.0 copy-start
  0.6 2.1 %copy-done = bf16[640,3072]{1,0:T(8,128)(2,1)S(1)} copy-done((bf16[640,3072]{1,0:T(8,128)(2,1)S(1)}, bf16[640,3072]{1,0:T(8,128)(2,1)}, u32[]{:S(2)}) %copy-start) | copy-done | bytes 3932184
  2.7 0.0 copy-start.1
  2.7 0.7 copy-done.1
  3.5 0.0 copy-start.2
  3.5 0.7 copy-done.2
  4.2 0.0 copy-start.3
  4.2 0.7 copy-done.3
  4.9 0.0 copy-start.4
  4.9 0.7 copy-done.4
  5.6 0.0 copy-start.5
  5.6 0.7 copy-done.5
  6.2 91.3 %window.1.normal = f32[64,640]{1,0:T(8,128)S(1)} custom-call(bf16[640,3072]{1,0:T(8,128)(2,1)S(1)} %copy-done, s32[5,24]{1,0:T(8,128)S(1)} %copy-done.4, f32[5,128]{1,0:T(8,128)S(1)} %bitcast.13, f32[1,3072]{1,0:T(1,128)S(1)} %bitcast.10, f32[1,3072]{1,0:T(1,128)S(1)} %bitcast.11, s32[1,3072]{1,0:T(1,128)S(1)} %bitcast.12), custom_call_target="tpu_custom_call" | custom-call | tf_op jit(solution)/shard_map/window/pallas_call | solution.py:427
  97.5 57.6 %gather.1 = (f32[16,32,640]{2,1,0:T(8,128)S(1)}, f32[32,16,512]{2,1,0:T(8,128)S(1)}, f32[2,16,512]{2,1,0:T(8,128)S(1)}) custom-call(f32[64,640]{1,0:T(8,128)S(1)} %window.1.normal), custom_call_target="tpu_custom_call" | custom-call | tf_op jit(solution)/shard_map/gather/pallas_call | solution.py:456
  155.1 52.4 %factor.1 = f32[64,640]{1,0:T(8,128)} custom-call(f32[64,640]{1,0:T(8,128)S(1)} %window.1.normal, f32[512,640]{1,0:T(8,128)S(1)} %bitcast.7, f32[512,512]{1,0:T(8,128)S(1)} %bitcast.8, f32[32,512]{1,0:T(8,128)S(1)} %bitcast.9), custom_call_target="tpu_custom_call" | custom-call | tf_op jit(solution)/shard_map/factor/pallas_call | solution.py:474
  207.5 0.7 copy.9
Async XLA Ops:
  0.6 2.1 %copy-start = (bf16[640,3072]{1,0:T(8,128)(2,1)S(1)}, bf16[640,3072]{1,0:T(8,128)(2,1)}, u32[]{:S(2)}) copy-start(bf16[640,3072]{1,0:T(8,128)(2,1)} %coef.1) | copy-start | bytes 11796484
  2.7 0.7 copy-start.1
  3.5 0.7 copy-start.2
  4.2 0.7 copy-start.3
  4.9 0.7 copy-start.4
  5.6 0.7 copy-start.5

commit v2 on v1

v2 whole, which is shorter than its diff:
```python
import functools

import jax
import jax.numpy as jnp
from jax import lax
from jax.experimental import pallas as pl
from jax.experimental.pallas import tpu as pltpu
from jax.sharding import PartitionSpec as P

PANEL = 512
SOFTNESS = 0.25
DIAGONAL_SHIFT = 0.5
CORES = 2
PLANES = 2
BLOCK = 128
MESH = pl.DeviceIdType.MESH
HIGHEST = lax.Precision.HIGHEST
NT = (((1,), (1,)), ((), ()))
NN = (((1,), (0,)), ((), ()))


def copy_to(src, dst, send_sem, recv_sem, g, c):
    return pltpu.make_async_remote_copy(
        src_ref=src, dst_ref=dst, send_sem=send_sem, recv_sem=recv_sem, device_id=(g, c), device_id_type=MESH
    )


class Place:
    def __init__(self, row_count, col_count):
        self.y_count = row_count // (CORES * PLANES)
        self.row_count, self.col_count = row_count, col_count
        self.g = lax.axis_index("grow")
        self.c = lax.axis_index("gcol")
        self.core = lax.rem(self.g, CORES)
        self.chip = self.g // CORES
        self.y = lax.rem(self.chip, self.y_count)
        self.plane = self.chip // self.y_count
        self.other = 1 - self.plane
        self.sibling = self.at(self.plane, self.y, 1 - self.core)
        self.partner = self.at(self.other, self.y, self.core)

    def at(self, plane, y, core):
        return (plane * self.y_count + y) * CORES + core

    def ring(self, hop):
        return lax.rem(self.y + hop + 2 * self.y_count, self.y_count)


def greet(me):
    barrier = pltpu.get_barrier_semaphore()
    for k in range(1, me.row_count):
        pl.semaphore_signal(barrier, inc=1, device_id=(lax.rem(me.g + k, me.row_count), me.c), device_id_type=MESH)
    for k in range(1, me.col_count):
        pl.semaphore_signal(barrier, inc=1, device_id=(me.g, lax.rem(me.c + k, me.col_count)), device_id_type=MESH)


def greeted(me):
    pl.semaphore_wait(pltpu.get_barrier_semaphore(), me.row_count + me.col_count - 2)


def window_kernel(
    row_count, col_count, panel_per,
    coef, mask_in, duals_in, costs_in, primal_in, fixed_in,
    normal, corner, epiece,
    a, win, mask, duals, costs, primal, fixed, dcol, pa, pb, scale, part, own, out, inc, qacc, qout, qin,
    load_sem, win_send, win_recv, pa_send, pa_recv, pb_send, pb_recv, rs_send, rs_recv, q_send, q_recv,
    t_send, t_recv, e_send, e_recv, cor_send, cor_recv,
):
    me = Place(row_count, col_count)
    rows, columns = a.shape
    window = 2 * panel_per
    tile_rows, tile_cols = mask.shape
    side = rows // tile_rows
    yc = me.y_count

    loads = [
        pltpu.make_async_copy(src, dst, load_sem.at[n])
        for n, (src, dst) in enumerate([
            (mask_in, mask),
            (coef.at[pl.ds(0, window)], a.at[pl.ds(0, window)]),
            (duals_in, duals),
            (coef.at[pl.ds(window, rows - window)], a.at[pl.ds(window, rows - window)]),
            (costs_in, costs), (primal_in, primal), (fixed_in, fixed),
        ])
    ]
    for load in loads:
        load.start()
    greet(me)
    loads[0].wait()
    loads[1].wait()

    def mask_window(k, _):
        sl = pl.ds(pl.multiple_of(k * side, side), side)
        m = mask[0, k].astype(jnp.float32)
        win[me.g, :, sl] = (a[0:window, sl].astype(jnp.float32) * m).astype(jnp.bfloat16)
        return 0

    lax.fori_loop(0, tile_cols, mask_window, 0)
    greeted(me)

    sends = []

    def send_window(slot, g):
        cp = copy_to(win.at[slot], win.at[slot], win_send.at[len(sends)], win_recv.at[slot], g, me.c)
        cp.start()
        sends.append(cp)

    def got_window(slot):
        copy_to(win.at[slot], win.at[slot], win_send.at[0], win_recv.at[slot], me.g, me.c).wait_recv()

    right = me.at(me.plane, me.ring(1), me.core)
    left = me.at(me.plane, me.ring(-1), me.core)
    reach = ((yc // 2, (yc - 1) // 2), ((yc - 1) // 2, yc // 2))
    planes = (me.plane, me.other)

    def pass_right(kind, hop):
        if hop < reach[kind][0]:
            send_window(me.at(planes[kind], me.ring(-hop), me.core), right)

    def pass_left(kind, hop):
        if hop < reach[kind][1]:
            send_window(me.at(planes[kind], me.ring(hop), me.core), left)

    send_window(me.g, me.partner)
    pass_right(0, 0)
    pass_left(0, 0)
    send_window(me.g, me.sibling)

    loads[2].wait()
    for i in range(tile_rows):
        dcol[i * side:(i + 1) * side, :] = jnp.transpose(jnp.broadcast_to(duals[i:i + 1, :], (side, side)))
    loads[3].wait()
    q = me.plane * CORES + me.core

    def products(k, _):
        sl = pl.ds(pl.multiple_of(k * side, side), side)
        total = jnp.zeros((8, side), jnp.float32)
        for i in range(tile_rows):
            block = slice(i * side, (i + 1) * side)
            x = a[block, sl].astype(jnp.float32) * mask[i, k].astype(jnp.float32)
            a[block, sl] = x.astype(jnp.bfloat16)
            total += (x * dcol[block, :]).reshape(side // 8, 8, side).sum(axis=0)
        pa[q, :, sl] = total.sum(axis=0, keepdims=True)
        return 0

    lax.fori_loop(0, tile_cols, products, 0)

    quad = [
        (lax.rem(me.plane + dp, PLANES), lax.rem(me.core + dc, CORES))
        for dp in range(PLANES) for dc in range(CORES) if dp or dc
    ]
    for n, (plane, core) in enumerate(quad):
        cp = copy_to(pa.at[q], pa.at[q], pa_send.at[n], pa_recv.at[q], me.at(plane, me.y, core), me.c)
        cp.start()

    got_window(me.partner)
    pass_right(1, 0)
    pass_left(1, 0)
    send_window(me.partner, me.sibling)

    for plane, core in quad:
        s = plane * CORES + core
        copy_to(pa.at[s], pa.at[s], pa_send.at[0], pa_recv.at[s], me.g, me.c).wait_recv()
    total = pa[0]
    for s in range(1, PLANES * CORES):
        total = total + pa[s]
    pb[me.y] = total
    small = []
    for k in range(1, yc):
        cp = copy_to(
            pb.at[me.y], pb.at[me.y], pb_send.at[k], pb_recv.at[me.y], me.at(me.plane, me.ring(k), me.core), me.c
        )
        cp.start()
        small.append(cp)

    def service(hop):
        for kind in (0, 1):
            if hop <= reach[kind][0]:
                slot = me.at(planes[kind], me.ring(-hop), me.core)
                got_window(slot)
                pass_right(kind, hop)
                send_window(slot, me.sibling)
            if hop <= reach[kind][1]:
                slot = me.at(planes[kind], me.ring(hop), me.core)
                got_window(slot)
                pass_left(kind, hop)
                send_window(slot, me.sibling)

    def chips_at(hop):
        chips = []
        for kind in (0, 1):
            if hop <= reach[kind][0]:
                chips.append((planes[kind], me.ring(-hop)))
            if hop and hop <= reach[kind][1]:
                chips.append((planes[kind], me.ring(hop)))
        return chips

    service(1)
    for k in range(1, yc):
        s = me.ring(k)
        copy_to(pb.at[s], pb.at[s], pb_send.at[0], pb_recv.at[s], me.g, me.c).wait_recv()
    total = pb[0]
    for s in range(1, yc):
        total = total + pb[s]
    for load in loads[4:]:
        load.wait()
    reduced = costs[...] - total
    scale[...] = (1 - fixed[...]).astype(jnp.float32) * primal[...] / jnp.sqrt(reduced * reduced + SOFTNESS)

    def rescale(k, _):
        sl = pl.ds(pl.multiple_of(k * side, side), side)
        s = jnp.broadcast_to(scale[:, sl], (side, side))
        for i in range(tile_rows):
            block = slice(i * side, (i + 1) * side)
            a[block, sl] = (a[block, sl].astype(jnp.float32) * s).astype(jnp.bfloat16)
        return 0

    lax.fori_loop(0, tile_cols, rescale, 0)

    blocks = row_count // col_count
    mine = blocks * window
    depth = min(512, columns)
    inc[me.c] = jnp.zeros(inc.shape[1:], inc.dtype)

    def multiply(chips):
        for plane, y in chips:
            @pl.when((plane * yc + y) != me.chip)
            def _():
                got_window(me.at(plane, y, 1 - me.core))

            @pl.when((plane * yc + y) == me.chip)
            def _():
                got_window(me.sibling)
        owners = [plane * yc + y for plane, y in chips]
        tall = len(owners) * mine
        part[0:tall, :] = jnp.zeros((tall, rows), jnp.float32)

        def deep(k, _):
            sl = pl.ds(pl.multiple_of(k * depth, depth), depth)
            lhs = jnp.concatenate(
                [win[pl.ds(o * blocks, blocks), :, sl].reshape(mine, depth) for o in owners], axis=0
            )
            part[0:tall, :] += lax.dot_general(lhs, a[:, sl], NT, preferred_element_type=jnp.float32)
            return 0

        lax.fori_loop(0, columns // depth, deep, 0)
        for k, owner in enumerate(owners):
            piece = part[k * mine:(k + 1) * mine, :]
            out[owner] = piece.astype(jnp.bfloat16)

            @pl.when(owner == me.c)
            def _():
                own[...] = piece

            @pl.when(owner != me.c)
            def _():
                copy_to(out.at[owner], inc.at[me.c], rs_send.at[owner], rs_recv.at[me.c], me.g, owner).start()

    last = yc // 2
    if last == 1:
        multiply(chips_at(0))
    for hop in range(2, last + 1):
        if hop == last:
            multiply(chips_at(hop - 1))
            service(hop)
        else:
            service(hop)
            if hop == 2:
                multiply(chips_at(0))
            multiply(chips_at(hop - 1))
    if last == 2:
        multiply(chips_at(0))
    multiply(chips_at(last))

    qacc[...] = jnp.zeros_like(qacc)

    def head(k, _):
        sl = pl.ds(pl.multiple_of(k * depth, depth), depth)
        rhs = win[:, 0:panel_per, sl].reshape(row_count * panel_per, depth)
        qacc[...] += lax.dot_general(a[0:window, sl], rhs, NT, preferred_element_type=jnp.float32)
        return 0

    lax.fori_loop(0, columns // depth, head, 0)
    wide = qacc.shape[1] // BLOCK
    half = col_count // 2
    for t in range(col_count):
        i, j = t // wide, t % wide
        qout[t] = qacc[8 * i:8 * i + 8, BLOCK * j:BLOCK * j + BLOCK]
    qin[me.c] = qout[me.c]
    for k in range(1, col_count):
        t = lax.rem(me.c + k, col_count)
        copy_to(qout.at[t], qin.at[me.c], q_send.at[k], q_recv.at[me.c], me.g, t).start()
    for k in range(1, col_count):
        s = lax.rem(me.c + k, col_count)
        copy_to(qin.at[s], qin.at[s], q_send.at[0], q_recv.at[s], me.g, me.c).wait_recv()
    tile = qin[0]
    for s in range(1, col_count):
        tile = tile + qin[s]

    in_corner = me.c < half
    home = me.chip

    @pl.when(in_corner)
    def _():
        corner[me.g, me.c] = tile
        for k in range(1, col_count):
            copy_to(
                corner.at[me.g, me.c], corner.at[me.g, me.c], t_send.at[k], t_recv.at[me.c],
                me.g, lax.rem(me.c + k, col_count),
            ).start()

    @pl.when(jnp.logical_not(in_corner))
    def _():
        epiece[me.c - half] = tile

        @pl.when(me.c != home)
        def _():
            copy_to(
                epiece.at[me.c - half], epiece.at[me.c - half], e_send.at[0], e_recv.at[me.c - half], me.g, home
            ).start()

    for s in range(half):
        @pl.when(me.c != s)
        def _():
            copy_to(corner.at[me.g, s], corner.at[me.g, s], t_send.at[0], t_recv.at[s], me.g, me.c).wait_recv()

    cor = []

    def send_corner(slot, g):
        cp = copy_to(corner.at[slot], corner.at[slot], cor_send.at[len(cor)], cor_recv.at[slot], g, me.c)
        cp.start()
        cor.append(cp)

    def got_corner(slot):
        copy_to(corner.at[slot], corner.at[slot], cor_send.at[0], cor_recv.at[slot], me.g, me.c).wait_recv()

    for k in range(1, yc):
        send_corner(me.g, me.at(me.plane, me.ring(k), me.core))
    send_corner(me.g, me.partner)
    send_corner(me.g, me.sibling)
    for k in range(1, yc):
        slot = me.at(me.plane, me.ring(k), me.core)
        got_corner(slot)
        send_corner(slot, me.partner)
        send_corner(slot, me.sibling)
    for k in range(yc):
        slot = me.at(me.other, me.ring(k), me.core)
        got_corner(slot)
        send_corner(slot, me.sibling)

    for s in range(col_count):
        @pl.when(me.c != s)
        def _():
            copy_to(out.at[s], inc.at[s], rs_send.at[s], rs_recv.at[s], me.g, me.c).wait_recv()

    total = own[...]
    for s in range(col_count):
        total = total + inc[s].astype(jnp.float32)
    normal[...] = total

    for plane in range(PLANES):
        for y in range(yc):
            got_corner(me.at(plane, y, 1 - me.core))

    @pl.when(me.c == home)
    def _():
        for t in range(half):
            @pl.when(me.c != half + t)
            def _():
                copy_to(epiece.at[t], epiece.at[t], e_send.at[0], e_recv.at[t], me.g, me.c).wait_recv()

    @pl.when(jnp.logical_not(in_corner) & (me.c != home))
    def _():
        copy_to(epiece.at[0], epiece.at[0], e_send.at[0], e_recv.at[0], me.g, home).wait_send()

    @pl.when(in_corner)
    def _():
        for k in range(1, col_count):
            copy_to(qout.at[0], qout.at[0], t_send.at[k], t_recv.at[0], me.g, me.c).wait_send()

    for s in range(col_count):
        @pl.when(me.c != s)
        def _():
            copy_to(out.at[s], inc.at[s], rs_send.at[s], rs_recv.at[s], me.g, me.c).wait_send()
    for k in range(1, col_count):
        copy_to(qout.at[0], qout.at[0], q_send.at[k], q_recv.at[0], me.g, me.c).wait_send()
    for n in range(len(quad)):
        copy_to(pa.at[0], pa.at[0], pa_send.at[n], pa_recv.at[0], me.g, me.c).wait_send()
    for cp in small + sends + cor:
        cp.wait_send()


def invert_block(d):
    n = d.shape[0]
    lane = lax.broadcasted_iota(jnp.int32, (8, n), 1)
    sub = lax.broadcasted_iota(jnp.int32, (8, n), 0)

    def spread(x):
        return jnp.broadcast_to(x, (8, n))

    rows = [d[8 * i:8 * i + 8, :] for i in range(n // 8)]
    done = []
    for b in range(n // 8):
        first = 8 * b
        cols = [spread(rows[b][:, first + k:first + k + 1]) for k in range(8)]
        inside = (lane >= first) & (lane < first + 8)
        w = jnp.where(inside, jnp.where(lane == sub + first, 1.0, 0.0), rows[b])
        lower = w
        scale = jnp.ones((8, n), jnp.float32)
        for k in range(8):
            ip = 1.0 / spread(cols[k][k:k + 1])
            scale = jnp.where(sub == k, ip, scale)
            lower = jnp.where(sub == k, w, lower)
            f = jnp.where(sub == k, 0.0, cols[k] * ip)
            w = w - f * spread(w[k:k + 1])
            for m in range(k + 1, 8):
                cols[m] = cols[m] - f * spread(cols[m][k:k + 1])
        w = w * scale
        done.append(jnp.where(lane <= sub + first, lower, 0.0) * jnp.sqrt(scale))
        ws = [spread(w[m:m + 1]) for m in range(8)]
        for i in range(b + 1, n // 8):
            left = jnp.where(inside, 0.0, rows[i])
            for m in range(8):
                left = left - spread(rows[i][:, first + m:first + m + 1]) * ws[m]
            rows[i] = left
    return jnp.concatenate(done, axis=0)


def dot32(x, y, dims=NN):
    return lax.dot_general(x, y, dims, precision=HIGHEST, preferred_element_type=jnp.float32)


def factor_kernel(
    row_count, col_count, panel_per,
    normal, corner, epiece,
    factor,
    s, panel, edge, panel_send, panel_recv, edge_send, edge_recv,
):
    me = Place(row_count, col_count)
    n = s.shape[0]
    own = n // col_count
    blocks = row_count // col_count
    greet(me)
    for b in range(blocks):
        panel[me.c, b * panel_per:(b + 1) * panel_per, :] = normal[2 * b * panel_per:(2 * b + 1) * panel_per, :]
    source = me.c == me.chip

    @pl.when(source)
    def _():
        edge[me.core] = epiece[...]

    greeted(me)
    peers = [
        me.at(plane, me.ring(k), me.core)
        for k in range(me.y_count) for plane in (me.plane, me.other)
    ][1:]

    def edge_copy(k, g):
        return copy_to(edge.at[me.core], edge.at[me.core], edge_send.at[k], edge_recv.at[me.core], g, me.c)

    @pl.when(source)
    def _():
        for k, peer in enumerate(peers):
            edge_copy(k, peer).start()

    sends = []
    for k in range(1, col_count):
        cp = copy_to(
            panel.at[me.c], panel.at[me.c], panel_send.at[k], panel_recv.at[me.c],
            me.g, lax.rem(me.c + k, col_count),
        )
        cp.start()
        sends.append(cp)

    row_id = lax.broadcasted_iota(jnp.int32, (n, n), 0)
    col_id = lax.broadcasted_iota(jnp.int32, (n, n), 1)
    wide = n // BLOCK
    high = panel_per // 8
    for i in range(high):
        for j in range(wide):
            t = i * wide + j
            for g in range(row_count):
                s[g * panel_per + 8 * i:g * panel_per + 8 * i + 8, j * BLOCK:(j + 1) * BLOCK] = corner[g, t]
    given = s[...]
    s[...] = 0.5 * (given + jnp.transpose(given)) + jnp.where(row_id == col_id, DIAGONAL_SHIFT, 0.0)

    def step(k, _):
        at = pl.ds(pl.multiple_of(k * BLOCK, BLOCK), BLOCK)
        inverse = invert_block(s[at, at])
        below = lax.broadcasted_iota(jnp.int32, (n, BLOCK), 0) >= (k + 1) * BLOCK
        column = jnp.where(below, dot32(s[:, at], inverse, NT), 0.0)
        s[at, at] = jnp.where(
            lax.broadcasted_iota(jnp.int32, (BLOCK, BLOCK), 0) == lax.broadcasted_iota(jnp.int32, (BLOCK, BLOCK), 1),
            1.0, 0.0,
        )
        row = dot32(inverse, s[at, :])
        s[at, :] = row
        s[:, at] = jnp.where(below, 0.0, s[:, at])
        s[...] = s[...] - dot32(column, row)

        @pl.when(k == 0)
        def _():
            @pl.when(jnp.logical_not(source))
            def _():
                edge_copy(0, me.g).wait_recv()

            edge_copy(len(peers), me.sibling).start()

        return 0

    lax.fori_loop(0, wide, step, 0)
    s[...] = jnp.where(col_id <= row_id, s[...], 0.0)
    inverse = s[...]
    across = 1 - me.core
    copy_to(edge.at[across], edge.at[across], edge_send.at[0], edge_recv.at[across], me.g, me.c).wait_recv()
    given_edge = jnp.concatenate(
        [edge[:, i * wide + j].reshape(CORES, 1, 8, BLOCK) for i in range(high) for j in range(wide)], axis=1
    )
    rows_edge = jnp.concatenate(
        [
            jnp.concatenate([given_edge[k, i * wide + j] for j in range(wide)], axis=1)
            for k in range(CORES) for i in range(high)
        ],
        axis=0,
    )
    turned = dot32(rows_edge, inverse, NT)
    weights = jnp.concatenate(
        [s[pl.ds(pl.multiple_of(me.c * own, own), own), :], dot32(turned, inverse)], axis=0
    )
    for k in range(1, col_count):
        t = lax.rem(me.c + k, col_count)
        copy_to(panel.at[t], panel.at[t], panel_send.at[0], panel_recv.at[t], me.g, me.c).wait_recv()
    made = dot32(weights, panel[...].reshape(n, panel.shape[2]))
    for b in range(blocks):
        at = b * panel_per
        factor[2 * at:2 * at + panel_per, :] = made[at:at + panel_per]
        factor[2 * at + panel_per:2 * at + 2 * panel_per, :] = (
            normal[2 * at + panel_per:2 * at + 2 * panel_per, :] - made[own + at:own + at + panel_per]
        )

    @pl.when(source)
    def _():
        for k, peer in enumerate(peers):
            edge_copy(k, peer).wait_send()

    edge_copy(len(peers), me.sibling).wait_send()
    for cp in sends:
        cp.wait_send()


def shards(row_count, col_count, coefficients, tile_mask, duals, costs, primal, fixed):
    rows, columns = coefficients.shape
    panel_per = PANEL // row_count
    window = 2 * panel_per
    blocks = row_count // col_count
    mine = blocks * window
    yc = row_count // (CORES * PLANES)
    half = col_count // 2
    own = PANEL // col_count
    assert blocks == CORES and half == (panel_per // 8) * (PANEL // BLOCK)
    vmem, anywhere = (pl.BlockSpec(memory_space=m) for m in (pltpu.VMEM, pl.ANY))
    dma = pltpu.SemaphoreType.DMA
    f32, bf16 = jnp.float32, jnp.bfloat16
    normal, corner, epiece = pl.pallas_call(
        functools.partial(window_kernel, row_count, col_count, panel_per),
        out_shape=(
            jax.ShapeDtypeStruct((mine, rows), f32),
            jax.ShapeDtypeStruct((row_count, half, 8, BLOCK), f32),
            jax.ShapeDtypeStruct((half, 8, BLOCK), f32),
        ),
        in_specs=[anywhere] * 6,
        out_specs=(vmem,) * 3,
        scratch_shapes=[
            pltpu.VMEM((rows, columns), bf16),
            pltpu.VMEM((row_count, window, columns), bf16),
            pltpu.SMEM(tile_mask.shape, jnp.int32),
            pltpu.VMEM((rows // BLOCK, BLOCK), f32),
            pltpu.VMEM((1, columns), f32), pltpu.VMEM((1, columns), f32), pltpu.VMEM((1, columns), jnp.int32),
            pltpu.VMEM((rows, BLOCK), f32),
            pltpu.VMEM((PLANES * CORES, 1, columns), f32),
            pltpu.VMEM((yc, 1, columns), f32),
            pltpu.VMEM((1, columns), f32),
            pltpu.VMEM((4 * mine, rows), f32),
            pltpu.VMEM((mine, rows), f32),
            pltpu.VMEM((col_count, mine, rows), bf16),
            pltpu.VMEM((col_count, mine, rows), bf16),
            pltpu.VMEM((window, PANEL), f32),
            pltpu.VMEM((col_count, 8, BLOCK), f32),
            pltpu.VMEM((col_count, 8, BLOCK), f32),
            dma((7,)),
            dma((row_count,)), dma((row_count,)),
            dma((PLANES * CORES,)), dma((PLANES * CORES,)),
            dma((yc,)), dma((yc,)),
            dma((col_count,)), dma((col_count,)),
            dma((col_count,)), dma((col_count,)),
            dma((col_count,)), dma((half,)),
            dma((1,)), dma((half,)),
            dma((row_count,)), dma((row_count,)),
        ],
        compiler_params=pltpu.CompilerParams(collective_id=0, has_side_effects=True, vmem_limit_bytes=40 << 20),
        name="window",
    )(
        coefficients, tile_mask, duals.reshape(rows // BLOCK, BLOCK), costs.reshape(1, columns),
        primal.reshape(1, columns), fixed.reshape(1, columns),
    )
    factor = pl.pallas_call(
        functools.partial(factor_kernel, row_count, col_count, panel_per),
        out_shape=jax.ShapeDtypeStruct((mine, rows), f32),
        in_specs=[vmem] * 3,
        out_specs=vmem,
        scratch_shapes=[
            pltpu.VMEM((PANEL, PANEL), f32),
            pltpu.VMEM((col_count, own, rows), f32),
            pltpu.VMEM((CORES, half, 8, BLOCK), f32),
            dma((col_count,)), dma((col_count,)),
            dma((row_count // 2,)), dma((CORES,)),
        ],
        compiler_params=pltpu.CompilerParams(collective_id=1, has_side_effects=True, vmem_limit_bytes=32 << 20),
        name="factor",
    )(normal, corner, epiece)
    return normal, factor


def solution(mesh):
    placed = (P("grow", "gcol"), P("grow", "gcol"), P("grow"), P("gcol"), P("gcol"), P("gcol"))
    return jax.shard_map(
        functools.partial(shards, mesh.shape["grow"], mesh.shape["gcol"]),
        mesh=mesh,
        in_specs=placed,
        out_specs=(P("gcol", "grow"), P("gcol", "grow")),
        check_vma=False,
    )
```

time: 209 us -> 144 us (0.69)
  Pallas kernels: 201 us -> 136 us
    pallas_call x2 -> x1, Pallas kernels: 110 us -> 40.4 us  [shards(): pl.pallas_call(functools.partial(factor_kernel, row_count, col_count, pan...]
    pallas_call x1, Pallas kernels: 91.3 us -> 95.3 us  [shards(): pl.pallas_call(functools.partial(window_kernel, row_count, col_count, pan...]
    unnamed x13 -> x14, local copies, waits for them, and re-layouts: 6.26 us -> 6.93 us
where the time goes in v2:
time: 144 us; the launch traced here: 143 us
  Pallas kernels  136 us (94%)
  local copies, waits for them, and re-layouts  6.93 us (5%)
    pallas_call x1, Pallas kernels, shards(): pl.pallas_call(functools.partial(window_kernel, row_count, col_count, pan...  95.3 us
    pallas_call x1, Pallas kernels, shards(): pl.pallas_call(functools.partial(factor_kernel, row_count, col_count, pan...  40.4 us
    unnamed x14, local copies, waits for them, and re-layouts  6.93 us

profile of v2, /device:TPU:6, one launch (start us, length us, event | category | flops | bytes accessed | tf_op | source)
XLA Modules:
  0.0 143.2 jit_solution(11363735779807562840)
XLA Ops:
  0.6 0.0 copy-start
  0.6 2.1 %copy-done = bf16[640,3072]{1,0:T(8,128)(2,1)S(1)} copy-done((bf16[640,3072]{1,0:T(8,128)(2,1)S(1)}, bf16[640,3072]{1,0:T(8,128)(2,1)}, u32[]{:S(2)}) %copy-start) | copy-done | bytes 3932184
  2.7 0.0 copy-start.1
  2.7 0.7 copy-done.1
  3.5 0.0 copy-start.2
  3.5 0.7 copy-done.2
  4.2 0.0 copy-start.3
  4.2 0.7 copy-done.3
  4.9 0.0 copy-start.4
  4.9 0.7 copy-done.4
  5.6 0.0 copy-start.5
  5.6 0.7 copy-done.5
  6.2 95.3 %window.1 = (f32[64,640]{1,0:T(8,128)S(1)}, f32[32,8,8,128]{3,2,1,0:T(8,128)S(1)}, f32[8,8,128]{2,1,0:T(8,128)S(1)}) custom-call(bf16[640,3072]{1,0:T(8,128)(2,1)S(1)} %copy-done, s32[5,24]{1,0:T(8,128)S(1)} %copy-done.4, f32[5,128]{1,0:T(8,128)S(1)} %bitcast.7, f32[1,3072]{1,0:T(1,128)S(1)} %bitcast.4, f32[1,3072]{1,0:T(1,128)S(1)} %bitcast.5, ...), custom_call_target="tpu_custom_call" | custom-call | tf_op jit(solution)/shard_map/window/pallas_call | solution.py:564
  101.5 40.4 %factor.1 = f32[64,640]{1,0:T(8,128)S(1)} custom-call(f32[64,640]{1,0:T(8,128)S(1)} %get-tuple-element.10.normal, f32[32,8,8,128]{3,2,1,0:T(8,128)S(1)} %get-tuple-element.6.corner, f32[8,8,128]{2,1,0:T(8,128)S(1)} %get-tuple-element.7.epiece), custom_call_target="tpu_custom_call" | custom-call | tf_op jit(solution)/shard_map/factor/pallas_call | solution.py:606
  141.9 0.7 copy.10
  142.5 0.7 copy.11
Async XLA Ops:
  0.6 2.1 %copy-start = (bf16[640,3072]{1,0:T(8,128)(2,1)S(1)}, bf16[640,3072]{1,0:T(8,128)(2,1)}, u32[]{:S(2)}) copy-start(bf16[640,3072]{1,0:T(8,128)(2,1)} %coef.1) | copy-start | bytes 11796484
  2.7 0.7 copy-start.1
  3.5 0.7 copy-start.2
  4.2 0.7 copy-start.3
  4.9 0.7 copy-start.4
  5.6 0.7 copy-start.5

commit v3 on v0

v3 whole, which is shorter than its diff:
```python
import functools

import jax
import jax.numpy as jnp
from jax import lax
from jax.experimental import pallas as pl
from jax.experimental.pallas import tpu as pltpu
from jax.sharding import PartitionSpec as P

PANEL = 512
SOFTNESS = 0.25
DIAGONAL_SHIFT = 0.5
CORES = 2
PLANES = 2
BLOCK = 128
MESH = pl.DeviceIdType.MESH
HIGHEST = lax.Precision.HIGHEST
NT = (((1,), (1,)), ((), ()))
NN = (((1,), (0,)), ((), ()))


def copy_to(src, dst, send_sem, recv_sem, g, c):
    return pltpu.make_async_remote_copy(
        src_ref=src, dst_ref=dst, send_sem=send_sem, recv_sem=recv_sem, device_id=(g, c), device_id_type=MESH
    )


class Place:
    def __init__(self, row_count, col_count):
        self.y_count = row_count // (CORES * PLANES)
        self.row_count, self.col_count = row_count, col_count
        self.g = lax.axis_index("grow")
        self.c = lax.axis_index("gcol")
        self.core = lax.rem(self.g, CORES)
        self.chip = self.g // CORES
        self.y = lax.rem(self.chip, self.y_count)
        self.plane = self.chip // self.y_count
        self.other = 1 - self.plane
        self.sibling = self.at(self.plane, self.y, 1 - self.core)
        self.partner = self.at(self.other, self.y, self.core)

    def at(self, plane, y, core):
        return (plane * self.y_count + y) * CORES + core

    def ring(self, hop):
        return lax.rem(self.y + hop + 2 * self.y_count, self.y_count)


def greet(me):
    barrier = pltpu.get_barrier_semaphore()
    for k in range(1, me.row_count):
        pl.semaphore_signal(barrier, inc=1, device_id=(lax.rem(me.g + k, me.row_count), me.c), device_id_type=MESH)
    for k in range(1, me.col_count):
        pl.semaphore_signal(barrier, inc=1, device_id=(me.g, lax.rem(me.c + k, me.col_count)), device_id_type=MESH)


def greeted(me):
    pl.semaphore_wait(pltpu.get_barrier_semaphore(), me.row_count + me.col_count - 2)


def invert_block(d):
    n = d.shape[0]
    lane = lax.broadcasted_iota(jnp.int32, (8, n), 1)
    sub = lax.broadcasted_iota(jnp.int32, (8, n), 0)

    def spread(x):
        return jnp.broadcast_to(x, (8, n))

    rows = [d[8 * i:8 * i + 8, :] for i in range(n // 8)]
    done = []
    for b in range(n // 8):
        first = 8 * b
        cols = [spread(rows[b][:, first + k:first + k + 1]) for k in range(8)]
        inside = (lane >= first) & (lane < first + 8)
        w = jnp.where(inside, jnp.where(lane == sub + first, 1.0, 0.0), rows[b])
        lower = w
        scale = jnp.ones((8, n), jnp.float32)
        for k in range(8):
            ip = 1.0 / spread(cols[k][k:k + 1])
            scale = jnp.where(sub == k, ip, scale)
            lower = jnp.where(sub == k, w, lower)
            f = jnp.where(sub == k, 0.0, cols[k] * ip)
            w = w - f * spread(w[k:k + 1])
            for m in range(k + 1, 8):
                cols[m] = cols[m] - f * spread(cols[m][k:k + 1])
        w = w * scale
        done.append(jnp.where(lane <= sub + first, lower, 0.0) * jnp.sqrt(scale))
        ws = [spread(w[m:m + 1]) for m in range(8)]
        for i in range(b + 1, n // 8):
            left = jnp.where(inside, 0.0, rows[i])
            for m in range(8):
                left = left - spread(rows[i][:, first + m:first + m + 1]) * ws[m]
            rows[i] = left
    return jnp.concatenate(done, axis=0)


def dot32(x, y, dims=NN):
    return lax.dot_general(x, y, dims, precision=HIGHEST, preferred_element_type=jnp.float32)


def step_kernel(
    row_count, col_count, panel_per,
    coef, mask_in, duals_in, costs_in, primal_in, fixed_in,
    normal, factor,
    a, win, mask, duals, costs, primal, fixed, dcol, pa, pb, scale, part, own, out, inc, qacc, qout, qin,
    corner, epiece, s, panel, edge,
    load_sem, win_send, win_recv, pa_send, pa_recv, pb_send, pb_recv, rs_send, rs_recv, q_send, q_recv,
    t_send, t_recv, e_send, e_recv, cor_send, cor_recv, panel_send, panel_recv, edge_send, edge_recv,
):
    me = Place(row_count, col_count)
    rows, columns = a.shape
    window = 2 * panel_per
    tile_rows, tile_cols = mask.shape
    side = rows // tile_rows
    yc = me.y_count
    last = yc // 2

    loads = [
        pltpu.make_async_copy(src, dst, load_sem.at[n])
        for n, (src, dst) in enumerate([
            (mask_in, mask),
            (coef.at[pl.ds(0, window)], a.at[pl.ds(0, window)]),
            (duals_in, duals),
            (coef.at[pl.ds(window, rows - window)], a.at[pl.ds(window, rows - window)]),
            (costs_in, costs), (primal_in, primal), (fixed_in, fixed),
        ])
    ]
    for load in loads:
        load.start()
    greet(me)
    loads[0].wait()
    loads[1].wait()

    def mask_window(k, _):
        sl = pl.ds(pl.multiple_of(k * side, side), side)
        m = mask[0, k].astype(jnp.float32)
        for h in (0, 1):
            win[h, me.g, :, sl] = (
                a[h * panel_per:(h + 1) * panel_per, sl].astype(jnp.float32) * m
            ).astype(jnp.bfloat16)
        return 0

    lax.fori_loop(0, tile_cols, mask_window, 0)
    greeted(me)

    sends = []

    def send_window(h, slot, g):
        cp = copy_to(win.at[h, slot], win.at[h, slot], win_send.at[len(sends)], win_recv.at[h, slot], g, me.c)
        cp.start()
        sends.append(cp)

    def got_window(h, slot):
        copy_to(win.at[h, slot], win.at[h, slot], win_send.at[0], win_recv.at[h, slot], me.g, me.c).wait_recv()

    right = me.at(me.plane, me.ring(1), me.core)
    left = me.at(me.plane, me.ring(-1), me.core)
    reach = ((last, (yc - 1) // 2), ((yc - 1) // 2, last))
    planes = (me.plane, me.other)

    def pass_right(h, kind, hop):
        if hop < reach[kind][0]:
            send_window(h, me.at(planes[kind], me.ring(-hop), me.core), right)

    def pass_left(h, kind, hop):
        if hop < reach[kind][1]:
            send_window(h, me.at(planes[kind], me.ring(hop), me.core), left)

    def begin(h):
        send_window(h, me.g, me.partner)
        pass_right(h, 0, 0)
        pass_left(h, 0, 0)
        send_window(h, me.g, me.sibling)

    def cross(h):
        got_window(h, me.partner)
        pass_right(h, 1, 0)
        pass_left(h, 1, 0)
        send_window(h, me.partner, me.sibling)

    def service(h, hop):
        for kind in (0, 1):
            if hop <= reach[kind][0]:
                slot = me.at(planes[kind], me.ring(-hop), me.core)
                got_window(h, slot)
                pass_right(h, kind, hop)
                send_window(h, slot, me.sibling)
            if hop <= reach[kind][1]:
                slot = me.at(planes[kind], me.ring(hop), me.core)
                got_window(h, slot)
                pass_left(h, kind, hop)
                send_window(h, slot, me.sibling)

    def chips_at(hop):
        chips = []
        for kind in (0, 1):
            if hop <= reach[kind][0]:
                chips.append((planes[kind], me.ring(-hop)))
            if hop and hop <= reach[kind][1]:
                chips.append((planes[kind], me.ring(hop)))
        return chips

    begin(0)

    loads[2].wait()
    for i in range(tile_rows):
        dcol[i * side:(i + 1) * side, :] = jnp.transpose(jnp.broadcast_to(duals[i:i + 1, :], (side, side)))
    loads[3].wait()
    q = me.plane * CORES + me.core

    def products(k, _):
        sl = pl.ds(pl.multiple_of(k * side, side), side)
        total = jnp.zeros((8, side), jnp.float32)
        for i in range(tile_rows):
            block = slice(i * side, (i + 1) * side)
            x = a[block, sl].astype(jnp.float32) * mask[i, k].astype(jnp.float32)
            a[block, sl] = x.astype(jnp.bfloat16)
            total += (x * dcol[block, :]).reshape(side // 8, 8, side).sum(axis=0)
        pa[q, :, sl] = total.sum(axis=0, keepdims=True)
        return 0

    lax.fori_loop(0, tile_cols, products, 0)

    quad = [
        (lax.rem(me.plane + dp, PLANES), lax.rem(me.core + dc, CORES))
        for dp in range(PLANES) for dc in range(CORES) if dp or dc
    ]
    for n, (plane, core) in enumerate(quad):
        copy_to(pa.at[q], pa.at[q], pa_send.at[n], pa_recv.at[q], me.at(plane, me.y, core), me.c).start()
    cross(0)
    for plane, core in quad:
        t = plane * CORES + core
        copy_to(pa.at[t], pa.at[t], pa_send.at[0], pa_recv.at[t], me.g, me.c).wait_recv()
    total = pa[0]
    for t in range(1, PLANES * CORES):
        total = total + pa[t]
    pb[me.y] = total
    small = []
    for k in range(1, yc):
        cp = copy_to(
            pb.at[me.y], pb.at[me.y], pb_send.at[k], pb_recv.at[me.y], me.at(me.plane, me.ring(k), me.core), me.c
        )
        cp.start()
        small.append(cp)

    for hop in range(1, last):
        service(0, hop)
    begin(1)
    for k in range(1, yc):
        t = me.ring(k)
        copy_to(pb.at[t], pb.at[t], pb_send.at[0], pb_recv.at[t], me.g, me.c).wait_recv()
    total = pb[0]
    for t in range(1, yc):
        total = total + pb[t]
    for load in loads[4:]:
        load.wait()
    reduced = costs[...] - total
    scale[...] = (1 - fixed[...]).astype(jnp.float32) * primal[...] / jnp.sqrt(reduced * reduced + SOFTNESS)

    def rescale(k, _):
        sl = pl.ds(pl.multiple_of(k * side, side), side)
        x = jnp.broadcast_to(scale[:, sl], (side, side))
        for i in range(tile_rows):
            block = slice(i * side, (i + 1) * side)
            a[block, sl] = (a[block, sl].astype(jnp.float32) * x).astype(jnp.bfloat16)
        return 0

    lax.fori_loop(0, tile_cols, rescale, 0)
    service(0, last)
    cross(1)
    for plane in range(PLANES):
        for y in range(yc):
            got_window(0, me.at(plane, y, 1 - me.core))

    blocks = row_count // col_count
    depth = min(512, columns)
    qacc[...] = jnp.zeros_like(qacc)

    def head(k, _):
        sl = pl.ds(pl.multiple_of(k * depth, depth), depth)
        rhs = win[0, :, :, sl].reshape(row_count * panel_per, depth)
        qacc[...] += lax.dot_general(a[0:window, sl], rhs, NT, preferred_element_type=jnp.float32)
        return 0

    lax.fori_loop(0, columns // depth, head, 0)
    n = s.shape[0]
    wide = n // BLOCK
    high = panel_per // 8
    half = col_count // 2
    for t in range(col_count):
        i, j = t // wide, t % wide
        qout[t] = qacc[8 * i:8 * i + 8, BLOCK * j:BLOCK * j + BLOCK]
    qin[me.c] = qout[me.c]
    for k in range(1, col_count):
        t = lax.rem(me.c + k, col_count)
        copy_to(qout.at[t], qin.at[me.c], q_send.at[k], q_recv.at[me.c], me.g, t).start()

    mine = blocks * panel_per
    for h in (0, 1):
        inc[h, me.c] = jnp.zeros(inc.shape[2:], inc.dtype)

    def multiply(h, owners):
        tall = len(owners) * mine
        part[0:tall, :] = jnp.zeros((tall, rows), jnp.float32)

        def deep(k, _):
            sl = pl.ds(pl.multiple_of(k * depth, depth), depth)
            lhs = jnp.concatenate(
                [win[h, pl.ds(o * blocks, blocks), :, sl].reshape(mine, depth) for o in owners], axis=0
            )
            part[0:tall, :] += lax.dot_general(lhs, a[:, sl], NT, preferred_element_type=jnp.float32)
            return 0

        lax.fori_loop(0, columns // depth, deep, 0)
        for k, owner in enumerate(owners):
            piece = part[k * mine:(k + 1) * mine, :]
            out[h, owner] = piece.astype(jnp.bfloat16)

            @pl.when(owner == me.c)
            def _():
                own[h] = piece

    def scatter(h, owners):
        for owner in owners:
            @pl.when(owner != me.c)
            def _():
                copy_to(
                    out.at[h, owner], inc.at[h, me.c], rs_send.at[h, owner], rs_recv.at[h, me.c], me.g, owner
                ).start()

    def multiply_trailing(hops):
        chips = [chip for hop in hops for chip in chips_at(hop)]
        for plane, y in chips:
            got_window(1, me.at(plane, y, 1 - me.core))
        if chips:
            multiply(1, [plane * yc + y for plane, y in chips])

    def gathered(h):
        for t in range(col_count):
            @pl.when(me.c != t)
            def _():
                copy_to(out.at[h, t], inc.at[h, t], rs_send.at[h, t], rs_recv.at[h, t], me.g, me.c).wait_recv()

        total = own[h]
        for t in range(col_count):
            total = total + inc[h, t].astype(jnp.float32)
        return total

    def trailing_service(hop):
        if hop <= last:
            service(1, hop)

    group = col_count // 2
    start = lax.rem(me.c, 2) * group
    owners = [start + k for k in range(group)]
    multiply(0, owners)
    scatter(0, owners)
    trailing_service(1)

    for k in range(1, col_count):
        t = lax.rem(me.c + k, col_count)
        copy_to(qin.at[t], qin.at[t], q_send.at[0], q_recv.at[t], me.g, me.c).wait_recv()
    tile = qin[0]
    for t in range(1, col_count):
        tile = tile + qin[t]
    in_corner = me.c < half
    home = me.chip

    @pl.when(in_corner)
    def _():
        corner[me.g, me.c] = tile
        for k in range(1, col_count):
            copy_to(
                corner.at[me.g, me.c], corner.at[me.g, me.c], t_send.at[k], t_recv.at[me.c],
                me.g, lax.rem(me.c + k, col_count),
            ).start()

    @pl.when(jnp.logical_not(in_corner))
    def _():
        epiece[me.c - half] = tile

        @pl.when(me.c != home)
        def _():
            copy_to(
                epiece.at[me.c - half], epiece.at[me.c - half], e_send.at[0], e_recv.at[me.c - half], me.g, home
            ).start()

    start = group - start
    owners = [start + k for k in range(group)]
    multiply(0, owners)
    scatter(0, owners)
    trailing_service(2)
    for t in range(half):
        @pl.when(me.c != t)
        def _():
            copy_to(corner.at[me.g, t], corner.at[me.g, t], t_send.at[0], t_recv.at[t], me.g, me.c).wait_recv()

    cor = []

    def send_corner(slot, g):
        cp = copy_to(corner.at[slot], corner.at[slot], cor_send.at[len(cor)], cor_recv.at[slot], g, me.c)
        cp.start()
        cor.append(cp)

    def got_corner(slot):
        copy_to(corner.at[slot], corner.at[slot], cor_send.at[0], cor_recv.at[slot], me.g, me.c).wait_recv()

    for k in range(1, yc):
        send_corner(me.g, me.at(me.plane, me.ring(k), me.core))
    send_corner(me.g, me.partner)
    send_corner(me.g, me.sibling)
    trailing_service(3)
    for k in range(1, yc):
        slot = me.at(me.plane, me.ring(k), me.core)
        got_corner(slot)
        send_corner(slot, me.partner)
        send_corner(slot, me.sibling)
    for hop in range(4, last + 1):
        trailing_service(hop)
    multiply_trailing(range(0, last - 1))
    for k in range(yc):
        slot = me.at(me.other, me.ring(k), me.core)
        got_corner(slot)
        send_corner(slot, me.sibling)
    multiply_trailing(range(last - 1, last + 1))

    source = me.c == home
    peers = [
        me.at(plane, me.ring(k), me.core) for k in range(yc) for plane in (me.plane, me.other)
    ][1:]

    def edge_copy(k, g):
        return copy_to(edge.at[me.core], edge.at[me.core], edge_send.at[k], edge_recv.at[me.core], g, me.c)

    @pl.when(source)
    def _():
        for t in range(half):
            @pl.when(me.c != half + t)
            def _():
                copy_to(epiece.at[t], epiece.at[t], e_send.at[0], e_recv.at[t], me.g, me.c).wait_recv()

        edge[me.core] = epiece[...]
        for k, peer in enumerate(peers):
            edge_copy(k, peer).start()

    panel[me.c] = gathered(0)
    zc = col_count // 2
    x_lo = lax.rem(me.c, 2)
    z = me.c // 2
    across = z * 2 + (1 - x_lo)
    far = []
    for k in range(1, zc // 2 + 1):
        far += [k, zc - k] if k != zc - k else [k]

    def send_panel(k, slot, c):
        copy_to(panel.at[slot], panel.at[slot], panel_send.at[k], panel_recv.at[slot], me.g, c).start()

    def got_panel(slot):
        copy_to(panel.at[slot], panel.at[slot], panel_send.at[0], panel_recv.at[slot], me.g, me.c).wait_recv()

    send_panel(0, me.c, across)
    for k in far:
        send_panel(k, me.c, lax.rem(z + k, zc) * 2 + x_lo)

    scatter(1, [lax.rem(me.c + k, col_count) for k in range(1, col_count)])

    def pass_panel(first, stop):
        for k in far[first:stop]:
            slot = lax.rem(z - k + zc, zc) * 2 + x_lo
            got_panel(slot)
            send_panel(zc + k, slot, across)

    for plane in range(PLANES):
        for y in range(yc):
            got_corner(me.at(plane, y, 1 - me.core))

    row_id = lax.broadcasted_iota(jnp.int32, (n, n), 0)
    col_id = lax.broadcasted_iota(jnp.int32, (n, n), 1)
    for i in range(high):
        for j in range(wide):
            t = i * wide + j
            for g in range(row_count):
                s[g * panel_per + 8 * i:g * panel_per + 8 * i + 8, j * BLOCK:(j + 1) * BLOCK] = corner[g, t]
    given = s[...]
    s[...] = 0.5 * (given + jnp.transpose(given)) + jnp.where(row_id == col_id, DIAGONAL_SHIFT, 0.0)

    def step(k, _):
        at = pl.ds(pl.multiple_of(k * BLOCK, BLOCK), BLOCK)
        inverse = invert_block(s[at, at])
        s[at, at] = inverse
        for m in range(wide):
            @pl.when(k == m)
            def _():
                lo, hi = m * BLOCK, (m + 1) * BLOCK
                inverse = s[lo:hi, lo:hi]
                if m:
                    s[lo:hi, 0:lo] = dot32(inverse, s[lo:hi, 0:lo])
                if hi < n:
                    column = dot32(s[hi:n, lo:hi], inverse, NT)
                    s[hi:n, lo:hi] = jnp.zeros((n - hi, BLOCK), jnp.float32)
                    s[lo:hi, hi:n] = dot32(inverse, s[lo:hi, hi:n])
                    s[hi:n, :] = s[hi:n, :] - dot32(column, s[lo:hi, :])

        cuts = [len(far) * m // 3 for m in range(4)]
        for m in range(min(3, wide)):
            @pl.when(k == m)
            def _():
                pass_panel(cuts[m], cuts[m + 1] if m + 1 < wide else len(far))
                if m == 0:
                    @pl.when(jnp.logical_not(source))
                    def _():
                        edge_copy(0, me.g).wait_recv()

                    edge_copy(len(peers), me.sibling).start()

        return 0

    lax.fori_loop(0, wide, step, 0)
    s[...] = jnp.where(col_id <= row_id, s[...], 0.0)
    inverse = s[...]
    over = 1 - me.core
    copy_to(edge.at[over], edge.at[over], edge_send.at[0], edge_recv.at[over], me.g, me.c).wait_recv()
    rows_edge = jnp.concatenate(
        [
            jnp.concatenate([edge[k, i * wide + j] for j in range(wide)], axis=1)
            for k in range(CORES) for i in range(high)
        ],
        axis=0,
    )
    turned = dot32(rows_edge, inverse, NT)
    weights = jnp.concatenate(
        [s[pl.ds(pl.multiple_of(me.c * mine, mine), mine), :], dot32(turned, inverse)], axis=0
    )
    for k in range(zc):
        got_panel(k * 2 + 1 - x_lo)
    made = dot32(weights, panel[...].reshape(n, rows))
    trailing = gathered(1)
    for b in range(blocks):
        at = b * panel_per
        p = slice(2 * at, 2 * at + panel_per)
        t = slice(2 * at + panel_per, 2 * at + 2 * panel_per)
        normal[p, :] = panel[me.c, at:at + panel_per, :]
        normal[t, :] = trailing[at:at + panel_per]
        factor[p, :] = made[at:at + panel_per]
        factor[t, :] = trailing[at:at + panel_per] - made[mine + at:mine + at + panel_per]

    @pl.when(source)
    def _():
        for k, peer in enumerate(peers):
            edge_copy(k, peer).wait_send()

    edge_copy(len(peers), me.sibling).wait_send()

    @pl.when(jnp.logical_not(in_corner) & (me.c != home))
    def _():
        copy_to(epiece.at[0], epiece.at[0], e_send.at[0], e_recv.at[0], me.g, home).wait_send()

    @pl.when(in_corner)
    def _():
        for k in range(1, col_count):
            copy_to(qout.at[0], qout.at[0], t_send.at[k], t_recv.at[0], me.g, me.c).wait_send()

    for h in (0, 1):
        for t in range(col_count):
            @pl.when(me.c != t)
            def _():
                copy_to(out.at[h, t], inc.at[h, t], rs_send.at[h, t], rs_recv.at[h, t], me.g, me.c).wait_send()
    for k in range(1, col_count):
        copy_to(qout.at[0], qout.at[0], q_send.at[k], q_recv.at[0], me.g, me.c).wait_send()
    for k in range(len(quad)):
        copy_to(pa.at[0], pa.at[0], pa_send.at[k], pa_recv.at[0], me.g, me.c).wait_send()
    for k in [0] + far + [zc + k for k in far]:
        copy_to(panel.at[0], panel.at[0], panel_send.at[k], panel_recv.at[0], me.g, me.c).wait_send()
    for cp in small + sends + cor:
        cp.wait_send()


def shards(row_count, col_count, coefficients, tile_mask, duals, costs, primal, fixed):
    rows, columns = coefficients.shape
    panel_per = PANEL // row_count
    window = 2 * panel_per
    blocks = row_count // col_count
    mine = blocks * panel_per
    yc = row_count // (CORES * PLANES)
    half = col_count // 2
    assert blocks == CORES and half == (panel_per // 8) * (PANEL // BLOCK)
    vmem, hbm = (pl.BlockSpec(memory_space=m) for m in (pltpu.VMEM, pltpu.HBM))
    dma = pltpu.SemaphoreType.DMA
    f32, bf16 = jnp.float32, jnp.bfloat16
    return pl.pallas_call(
        functools.partial(step_kernel, row_count, col_count, panel_per),
        out_shape=(jax.ShapeDtypeStruct((2 * mine, rows), f32),) * 2,
        in_specs=[hbm] * 6,
        out_specs=(vmem,) * 2,
        scratch_shapes=[
            pltpu.VMEM((rows, columns), bf16),
            pltpu.VMEM((2, row_count, panel_per, columns), bf16),
            pltpu.SMEM(tile_mask.shape, jnp.int32),
            pltpu.VMEM((rows // BLOCK, BLOCK), f32),
            pltpu.VMEM((1, columns), f32), pltpu.VMEM((1, columns), f32), pltpu.VMEM((1, columns), jnp.int32),
            pltpu.VMEM((rows, BLOCK), f32),
            pltpu.VMEM((PLANES * CORES, 1, columns), f32),
            pltpu.VMEM((yc, 1, columns), f32),
            pltpu.VMEM((1, columns), f32),
            pltpu.VMEM((col_count * mine, rows), f32),
            pltpu.VMEM((2, mine, rows), f32),
            pltpu.VMEM((2, col_count, mine, rows), bf16),
            pltpu.VMEM((2, col_count, mine, rows), bf16),
            pltpu.VMEM((window, PANEL), f32),
            pltpu.VMEM((col_count, 8, BLOCK), f32),
            pltpu.VMEM((col_count, 8, BLOCK), f32),
            pltpu.VMEM((row_count, half, 8, BLOCK), f32),
            pltpu.VMEM((half, 8, BLOCK), f32),
            pltpu.VMEM((PANEL, PANEL), f32),
            pltpu.VMEM((col_count, mine, rows), f32),
            pltpu.VMEM((CORES, half, 8, BLOCK), f32),
            dma((7,)),
            dma((2 * row_count,)), dma((2, row_count)),
            dma((PLANES * CORES,)), dma((PLANES * CORES,)),
            dma((yc,)), dma((yc,)),
            dma((2, col_count)), dma((2, col_count)),
            dma((col_count,)), dma((col_count,)),
            dma((col_count,)), dma((half,)),
            dma((1,)), dma((half,)),
            dma((row_count,)), dma((row_count,)),
            dma((col_count,)), dma((col_count,)),
            dma((row_count // 2,)), dma((CORES,)),
        ],
        compiler_params=pltpu.CompilerParams(collective_id=0, has_side_effects=True, vmem_limit_bytes=60 << 20),
        name="window_step",
    )(
        coefficients, tile_mask, duals.reshape(rows // BLOCK, BLOCK), costs.reshape(1, columns),
        primal.reshape(1, columns), fixed.reshape(1, columns),
    )


def solution(mesh):
    placed = (P("grow", "gcol"), P("grow", "gcol"), P("grow"), P("gcol"), P("gcol"), P("gcol"))
    return jax.shard_map(
        functools.partial(shards, mesh.shape["grow"], mesh.shape["gcol"]),
        mesh=mesh,
        in_specs=placed,
        out_specs=(P("gcol", "grow"), P("gcol", "grow")),
        check_vma=False,
    )
```

time: 648 us -> 119 us (0.18); the launches traced: 640 us -> 118 us
  waiting for transfers between devices: 315 us -> 0 us
  blocking collectives: 133 us -> 0 us
  other arithmetic: 125 us -> 0 us
  Pallas kernels: 0 us -> 114 us
  matrix products: 25.4 us -> 0 us
  local copies, waits for them, and re-layouts: 23.3 us -> 3.18 us
  between operations: 16.8 us -> 0.64 us
    all_gather x4 -> x0, waiting for transfers between devices: 237 us -> none  [the longest x1 83 us: shards(): lax.all_gather(panel_all[:, :panel_per], 'grow', axis=1, tiled=True)]
    psum x1 -> x0, blocking collectives: 133 us -> none  [shards(): products = lax.psum(partial_products, 'grow')]
    another operation x19 -> x0, other arithmetic: 123 us -> none  [the longest x14 83.1 us: shards(): lower = jnp.linalg.cholesky(shifted)]
    pallas_call x0 -> x1, Pallas kernels: none -> 114 us  [shards(): pl.pallas_call(functools.partial(step_kernel, row_count, col_count, panel...]
    reduce_scatter x1 -> x0, waiting for transfers between devices: 78.7 us -> none  [shards(): lax.psum_scatter(lax.dot_general(window_all, scaled, (((1,), (1,)), ((),...]
    dot_general x3 -> x0, matrix products: 14.9 us -> none  [the longest x1 9.47 us: shards(): lax.dot_general(window_all, scaled, (((1,), (1,)), ((), ())), preferred_e...]
    another operation x18 -> x0, local copies, waits for them, and re-layouts: 13 us -> none
    another operation x13 -> x0, matrix products: 10.5 us -> none  [the longest x7 6.24 us: shards(): jax.scipy.linalg.solve_triangular(lower, panel_all, lower=True)]
  transfers between devices with their start and end apart: 5 -> 0, of which waited for: 4 -> 0; matrix products, arithmetic and copies ran while one was open for 1% -> 0% of each run, Pallas kernels for 0% -> 0%
where the time goes in v3:
time: 119 us; the launch traced here: 118 us
  Pallas kernels  114 us (96%)
  local copies, waits for them, and re-layouts  3.18 us (3%)
    pallas_call x1, Pallas kernels, shards(): pl.pallas_call(functools.partial(step_kernel, row_count, col_count, panel...  114 us
    unnamed x2, local copies, waits for them, and re-layouts  3.18 us

profile of v3, /device:TPU:6, one launch (start us, length us, event | category | flops | bytes accessed | tf_op | source)
XLA Modules:
  0.0 117.8 jit_solution(12384695138943116695)
XLA Ops:
  0.6 114.0 %window_step.1 = (f32[64,640]{1,0:T(8,128)}, f32[64,640]{1,0:T(8,128)}) custom-call(bf16[640,3072]{1,0:T(8,128)(2,1)} %coef.1, s32[5,24]{1,0:T(8,128)} %mask_in.1, f32[5,128]{1,0:T(8,128)} %bitcast.7, f32[1,3072]{1,0:T(1,128)} %bitcast.4, f32[1,3072]{1,0:T(1,128)} %bitcast.5, s32[1,3072]{1,0:T(1,128)} %bitcast.6), custom_call_target="tpu_custom_call" | custom-call | tf_op jit(solution)/shard_map/window_step/pallas_call | solution.py:590
  114.6 1.6 %copy.10 = f32[64,640]{1,0:T(8,128)} copy(f32[64,640]{1,0:T(8,128)} %get-tuple-element.4) | data formatting | bytes 327680
  116.2 1.6 %copy.11 = f32[64,640]{1,0:T(8,128)} copy(f32[64,640]{1,0:T(8,128)} %get-tuple-element.5) | data formatting | bytes 327680

commit v4 on v3

--- a/solution.py
+++ b/solution.py
@@ -102,9 +102,10 @@
     row_count, col_count, panel_per,
     coef, mask_in, duals_in, costs_in, primal_in, fixed_in,
     normal, factor,
-    a, win, mask, duals, costs, primal, fixed, dcol, pa, pb, scale, part, own, out, inc, qacc, qout, qin,
+    a, win, mask, duals, costs, primal, fixed, dcol, pa, pb, scale, part, pair, out_x, in_x, out_z, in_z,
+    qacc, qout, qin,
     corner, epiece, s, panel, edge,
-    load_sem, win_send, win_recv, pa_send, pa_recv, pb_send, pb_recv, rs_send, rs_recv, q_send, q_recv,
+    load_sem, win_send, win_recv, pa_send, pa_recv, pb_send, pb_recv, x_send, x_recv, z_send, z_recv, q_send, q_recv,
     t_send, t_recv, e_send, e_recv, cor_send, cor_recv, panel_send, panel_recv, edge_send, edge_recv,
 ):
     me = Place(row_count, col_count)
@@ -190,15 +191,6 @@
                 got_window(h, slot)
                 pass_left(h, kind, hop)
                 send_window(h, slot, me.sibling)
-
-    def chips_at(hop):
-        chips = []
-        for kind in (0, 1):
-            if hop <= reach[kind][0]:
-                chips.append((planes[kind], me.ring(-hop)))
-            if hop and hop <= reach[kind][1]:
-                chips.append((planes[kind], me.ring(hop)))
-        return chips
 
     begin(0)
 
@@ -296,66 +288,61 @@
         copy_to(qout.at[t], qin.at[me.c], q_send.at[k], q_recv.at[me.c], me.g, t).start()
 
     mine = blocks * panel_per
-    for h in (0, 1):
-        inc[h, me.c] = jnp.zeros(inc.shape[2:], inc.dtype)
-
-    def multiply(h, owners):
-        tall = len(owners) * mine
-        part[0:tall, :] = jnp.zeros((tall, rows), jnp.float32)
+    zc = col_count // 2
+    x_lo = lax.rem(me.c, 2)
+    z = me.c // 2
+    across = z * 2 + (1 - x_lo)
+
+    def multiply(h, x):
+        part[...] = jnp.zeros_like(part)
 
         def deep(k, _):
             sl = pl.ds(pl.multiple_of(k * depth, depth), depth)
             lhs = jnp.concatenate(
-                [win[h, pl.ds(o * blocks, blocks), :, sl].reshape(mine, depth) for o in owners], axis=0
+                [win[h, pl.ds((t * 2 + x) * blocks, blocks), :, sl].reshape(mine, depth) for t in range(zc)], axis=0
             )
-            part[0:tall, :] += lax.dot_general(lhs, a[:, sl], NT, preferred_element_type=jnp.float32)
+            part[...] += lax.dot_general(lhs, a[:, sl], NT, preferred_element_type=jnp.float32)
             return 0
 
         lax.fori_loop(0, columns // depth, deep, 0)
-        for k, owner in enumerate(owners):
-            piece = part[k * mine:(k + 1) * mine, :]
-            out[h, owner] = piece.astype(jnp.bfloat16)
-
-            @pl.when(owner == me.c)
-            def _():
-                own[h] = piece
-
-    def scatter(h, owners):
-        for owner in owners:
-            @pl.when(owner != me.c)
-            def _():
-                copy_to(
-                    out.at[h, owner], inc.at[h, me.c], rs_send.at[h, owner], rs_recv.at[h, me.c], me.g, owner
-                ).start()
-
-    def multiply_trailing(hops):
-        chips = [chip for hop in hops for chip in chips_at(hop)]
-        for plane, y in chips:
-            got_window(1, me.at(plane, y, 1 - me.core))
-        if chips:
-            multiply(1, [plane * yc + y for plane, y in chips])
+
+    def pair_copy(h):
+        return copy_to(out_x.at[h], in_x.at[h], x_send.at[h], x_recv.at[h], me.g, across)
+
+    def scatter_pair(h):
+        multiply(h, 1 - x_lo)
+        for t in range(zc):
+            out_x[h, t] = part[t * mine:(t + 1) * mine, :].astype(jnp.bfloat16)
+        pair_copy(h).start()
+
+    def keep(h):
+        multiply(h, x_lo)
+        for t in range(zc):
+            pair[h, t] = part[t * mine:(t + 1) * mine, :]
+
+    def scatter(h):
+        pair_copy(h).wait_recv()
+        for t in range(zc):
+            both = pair[h, t] + in_x[h, t].astype(jnp.float32)
+            pair[h, t] = both
+            out_z[h, t] = both.astype(jnp.bfloat16)
+        for k in range(1, zc):
+            t = lax.rem(z + k, zc)
+            copy_to(out_z.at[h, t], in_z.at[h, z], z_send.at[h, t], z_recv.at[h, z], me.g, t * 2 + x_lo).start()
 
     def gathered(h):
-        for t in range(col_count):
-            @pl.when(me.c != t)
-            def _():
-                copy_to(out.at[h, t], inc.at[h, t], rs_send.at[h, t], rs_recv.at[h, t], me.g, me.c).wait_recv()
-
-        total = own[h]
-        for t in range(col_count):
-            total = total + inc[h, t].astype(jnp.float32)
+        total = pair[h, z]
+        for k in range(1, zc):
+            t = lax.rem(z + k, zc)
+            copy_to(out_z.at[h, t], in_z.at[h, t], z_send.at[h, t], z_recv.at[h, t], me.g, me.c).wait_recv()
+            total = total + in_z[h, t].astype(jnp.float32)
         return total
 
     def trailing_service(hop):
         if hop <= last:
             service(1, hop)
 
-    group = col_count // 2
-    start = lax.rem(me.c, 2) * group
-    owners = [start + k for k in range(group)]
-    multiply(0, owners)
-    scatter(0, owners)
-    trailing_service(1)
+    scatter_pair(0)
 
     for k in range(1, col_count):
         t = lax.rem(me.c + k, col_count)
@@ -385,10 +372,9 @@
                 epiece.at[me.c - half], epiece.at[me.c - half], e_send.at[0], e_recv.at[me.c - half], me.g, home
             ).start()
 
-    start = group - start
-    owners = [start + k for k in range(group)]
-    multiply(0, owners)
-    scatter(0, owners)
+    trailing_service(1)
+    keep(0)
+    scatter(0)
     trailing_service(2)
     for t in range(half):
         @pl.when(me.c != t)
@@ -415,14 +401,10 @@
         got_corner(slot)
         send_corner(slot, me.partner)
         send_corner(slot, me.sibling)
-    for hop in range(4, last + 1):
-        trailing_service(hop)
-    multiply_trailing(range(0, last - 1))
     for k in range(yc):
         slot = me.at(me.other, me.ring(k), me.core)
         got_corner(slot)
         send_corner(slot, me.sibling)
-    multiply_trailing(range(last - 1, last + 1))
 
     source = me.c == home
     peers = [
@@ -444,10 +426,6 @@
             edge_copy(k, peer).start()
 
     panel[me.c] = gathered(0)
-    zc = col_count // 2
-    x_lo = lax.rem(me.c, 2)
-    z = me.c // 2
-    across = z * 2 + (1 - x_lo)
     far = []
     for k in range(1, zc // 2 + 1):
         far += [k, zc - k] if k != zc - k else [k]
@@ -462,7 +440,6 @@
     for k in far:
         send_panel(k, me.c, lax.rem(z + k, zc) * 2 + x_lo)
 
-    scatter(1, [lax.rem(me.c + k, col_count) for k in range(1, col_count)])
 
     def pass_panel(first, stop):
         for k in far[first:stop]:
@@ -473,6 +450,8 @@
     for plane in range(PLANES):
         for y in range(yc):
             got_corner(me.at(plane, y, 1 - me.core))
+    for hop in range(4, last + 1):
+        trailing_service(hop)
 
     row_id = lax.broadcasted_iota(jnp.int32, (n, n), 0)
     col_id = lax.broadcasted_iota(jnp.int32, (n, n), 1)
@@ -512,6 +491,18 @@
                         edge_copy(0, me.g).wait_recv()
 
                     edge_copy(len(peers), me.sibling).start()
+
+        @pl.when(k == 0)
+        def _():
+            for plane in range(PLANES):
+                for y in range(yc):
+                    got_window(1, me.at(plane, y, 1 - me.core))
+            scatter_pair(1)
+
+        @pl.when(k == min(1, wide - 1))
+        def _():
+            keep(1)
+            scatter(1)
 
         return 0
 
@@ -561,10 +552,10 @@
             copy_to(qout.at[0], qout.at[0], t_send.at[k], t_recv.at[0], me.g, me.c).wait_send()
 
     for h in (0, 1):
-        for t in range(col_count):
-            @pl.when(me.c != t)
-            def _():
-                copy_to(out.at[h, t], inc.at[h, t], rs_send.at[h, t], rs_recv.at[h, t], me.g, me.c).wait_send()
+        pair_copy(h).wait_send()
+        for k in range(1, zc):
+            t = lax.rem(z + k, zc)
+            copy_to(out_z.at[h, t], in_z.at[h, t], z_send.at[h, t], z_recv.at[h, t], me.g, me.c).wait_send()
     for k in range(1, col_count):
         copy_to(qout.at[0], qout.at[0], q_send.at[k], q_recv.at[0], me.g, me.c).wait_send()
     for k in range(len(quad)):
@@ -602,10 +593,12 @@
             pltpu.VMEM((PLANES * CORES, 1, columns), f32),
             pltpu.VMEM((yc, 1, columns), f32),
             pltpu.VMEM((1, columns), f32),
-            pltpu.VMEM((col_count * mine, rows), f32),
-            pltpu.VMEM((2, mine, rows), f32),
-            pltpu.VMEM((2, col_count, mine, rows), bf16),
-            pltpu.VMEM((2, col_count, mine, rows), bf16),
+            pltpu.VMEM((half * mine, rows), f32),
+            pltpu.VMEM((2, half, mine, rows), f32),
+            pltpu.VMEM((2, half, mine, rows), bf16),
+            pltpu.VMEM((2, half, mine, rows), bf16),
+            pltpu.VMEM((2, half, mine, rows), bf16),
+            pltpu.VMEM((2, half, mine, rows), bf16),
             pltpu.VMEM((window, PANEL), f32),
             pltpu.VMEM((col_count, 8, BLOCK), f32),
             pltpu.VMEM((col_count, 8, BLOCK), f32),
@@ -618,7 +611,8 @@
             dma((2 * row_count,)), dma((2, row_count)),
             dma((PLANES * CORES,)), dma((PLANES * CORES,)),
             dma((yc,)), dma((yc,)),
-            dma((2, col_count)), dma((2, col_count)),
+            dma((2,)), dma((2,)),
+            dma((2, half)), dma((2, half)),
             dma((col_count,)), dma((col_count,)),
             dma((col_count,)), dma((half,)),
             dma((1,)), dma((half,)),

time: 119 us -> 114 us (0.958)
  Pallas kernels: 114 us -> 110 us
    pallas_call x1, Pallas kernels: 114 us -> 110 us  [shards(): pl.pallas_call(functools.partial(step_kernel, row_count, col_count, panel...]
where the time goes in v4:
time: 114 us
  Pallas kernels  110 us (96%)
  local copies, waits for them, and re-layouts  3.18 us (3%)
    pallas_call x1, Pallas kernels, shards(): pl.pallas_call(functools.partial(step_kernel, row_count, col_count, panel...  110 us
    unnamed x2, local copies, waits for them, and re-layouts  3.18 us

profile of v4, /device:TPU:6, one launch (start us, length us, event | category | flops | bytes accessed | tf_op | source)
XLA Modules:
  0.0 113.6 jit_solution(12175993223387303978)
XLA Ops:
  0.6 109.8 %window_step.1 = (f32[64,640]{1,0:T(8,128)}, f32[64,640]{1,0:T(8,128)}) custom-call(bf16[640,3072]{1,0:T(8,128)(2,1)} %coef.1, s32[5,24]{1,0:T(8,128)} %mask_in.1, f32[5,128]{1,0:T(8,128)} %bitcast.7, f32[1,3072]{1,0:T(1,128)} %bitcast.4, f32[1,3072]{1,0:T(1,128)} %bitcast.5, s32[1,3072]{1,0:T(1,128)} %bitcast.6), custom_call_target="tpu_custom_call" | custom-call | tf_op jit(solution)/shard_map/window_step/pallas_call | solution.py:581
  110.5 1.6 %copy.10 = f32[64,640]{1,0:T(8,128)} copy(f32[64,640]{1,0:T(8,128)} %get-tuple-element.4) | data formatting | bytes 327680
  112.1 1.6 %copy.11 = f32[64,640]{1,0:T(8,128)} copy(f32[64,640]{1,0:T(8,128)} %get-tuple-element.5) | data formatting | bytes 327680

commit v5 on v4

--- a/solution.py
+++ b/solution.py
@@ -309,11 +309,10 @@
     def pair_copy(h):
         return copy_to(out_x.at[h], in_x.at[h], x_send.at[h], x_recv.at[h], me.g, across)
 
-    def scatter_pair(h):
+    def make_pair(h):
         multiply(h, 1 - x_lo)
         for t in range(zc):
             out_x[h, t] = part[t * mine:(t + 1) * mine, :].astype(jnp.bfloat16)
-        pair_copy(h).start()
 
     def keep(h):
         multiply(h, x_lo)
@@ -342,7 +341,7 @@
         if hop <= last:
             service(1, hop)
 
-    scatter_pair(0)
+    make_pair(0)
 
     for k in range(1, col_count):
         t = lax.rem(me.c + k, col_count)
@@ -372,10 +371,9 @@
                 epiece.at[me.c - half], epiece.at[me.c - half], e_send.at[0], e_recv.at[me.c - half], me.g, home
             ).start()
 
+    pair_copy(0).start()
     trailing_service(1)
     keep(0)
-    scatter(0)
-    trailing_service(2)
     for t in range(half):
         @pl.when(me.c != t)
         def _():
@@ -395,6 +393,8 @@
         send_corner(me.g, me.at(me.plane, me.ring(k), me.core))
     send_corner(me.g, me.partner)
     send_corner(me.g, me.sibling)
+    trailing_service(2)
+    scatter(0)
     trailing_service(3)
     for k in range(1, yc):
         slot = me.at(me.plane, me.ring(k), me.core)
@@ -497,7 +497,8 @@
             for plane in range(PLANES):
                 for y in range(yc):
                     got_window(1, me.at(plane, y, 1 - me.core))
-            scatter_pair(1)
+            make_pair(1)
+            pair_copy(1).start()
 
         @pl.when(k == min(1, wide - 1))
         def _():

time: 114 us -> 113 us (level); the launches traced: 114 us -> 111 us
  Pallas kernels: 110 us -> 107 us
    pallas_call x1, Pallas kernels: 110 us -> 107 us  [shards(): pl.pallas_call(functools.partial(step_kernel, row_count, col_count, panel...]
where the time goes in v5:
time: 113 us; the launch traced here: 111 us
  Pallas kernels  107 us (95%)
  local copies, waits for them, and re-layouts  3.18 us (3%)
    pallas_call x1, Pallas kernels, shards(): pl.pallas_call(functools.partial(step_kernel, row_count, col_count, panel...  107 us
    unnamed x2, local copies, waits for them, and re-layouts  3.18 us

profile of v5, /device:TPU:6, one launch (start us, length us, event | category | flops | bytes accessed | tf_op | source)
XLA Modules:
  0.0 111.3 jit_solution(6805265549543386439)
XLA Ops:
  0.6 107.5 %window_step.1 = (f32[64,640]{1,0:T(8,128)}, f32[64,640]{1,0:T(8,128)}) custom-call(bf16[640,3072]{1,0:T(8,128)(2,1)} %coef.1, s32[5,24]{1,0:T(8,128)} %mask_in.1, f32[5,128]{1,0:T(8,128)} %bitcast.7, f32[1,3072]{1,0:T(1,128)} %bitcast.4, f32[1,3072]{1,0:T(1,128)} %bitcast.5, s32[1,3072]{1,0:T(1,128)} %bitcast.6), custom_call_target="tpu_custom_call" | custom-call | tf_op jit(solution)/shard_map/window_step/pallas_call | solution.py:582
  108.1 1.6 %copy.10 = f32[64,640]{1,0:T(8,128)} copy(f32[64,640]{1,0:T(8,128)} %get-tuple-element.4) | data formatting | bytes 327680
  109.7 1.6 %copy.11 = f32[64,640]{1,0:T(8,128)} copy(f32[64,640]{1,0:T(8,128)} %get-tuple-element.5) | data formatting | bytes 327680
